TPU v7x, 256 devices: a whole 4x4x8 slice. The times are simulated.
256 devices in a mesh: seq: 32 (over y, x, core), tensor: 8 (over z).
Axes of the slice: x: 4, y: 4, z: 8, core: 2. Of those that a mesh axis runs over, the one named last changes fastest.
Arguments:
- queries: bfloat16 [4096, 8192], P('seq', 'tensor'), may hold values from -6 to 6
- key_vectors: bfloat16 [4096, 8192], P('seq', 'tensor'), may hold values from -6 to 6
- value_rows: bfloat16 [4096, 8192], P('seq', 'tensor'), may hold values from -6 to 6
- gate_logits: bfloat16 [4096, 8192], P('seq', 'tensor'), may hold values from -6 to 6
- log_decay: float32 [4096, 64], P('seq', 'tensor'), may hold values from -0.73 to 0, as said below
- initial_state: float32 [64, 128, 128], P('tensor'), may hold values from -192 to 192
- norm_gain: float32 [8192], P('tensor'), may hold values from 0.25 to 1.75
- out_weight: bfloat16 [8192, 6144], P('tensor', 'seq'), may hold values from -0.0625 to 0.0625
Outputs:
- mixed: float32 [4096, 6144], P('seq', 'tensor')
Inputs may be any that keep to these rules, and one draw needn't show every extreme that they name: `log_decay`: every entry is negative.
All inputs are finite; a program needn't handle non-finite values.
Results may differ from a plain program's by a relative error of at most 0.0075.
Values may be sent and summed in bfloat16 or wider, within the bound.
No kernel may reach another device: no remote copies, remote signals or barrier semaphores. Data moves between devices by JAX's collectives and lax.ppermute only.
A program may use at most 128 MiB of HBM per device.

v0:
```python
import jax
import jax.numpy as jnp
from jax import lax
from jax.sharding import PartitionSpec as P

HIGH = lax.Precision.HIGHEST


def entering(array, axis, combine, identity):
    length, mine = (lax.axis_size(axis), lax.axis_index(axis))
    everything = jax.tree.map(lambda part: lax.all_gather(part, axis), array)
    start = jax.tree.map(
        lambda part, zero: jnp.broadcast_to(jnp.asarray(zero, part.dtype), part.shape),
        array,
        identity,
    )

    def hop(k, before):
        reached = k < mine
        new = combine(before, jax.tree.map(lambda part: part[k], everything))
        return jax.tree.map(lambda a, b: jnp.where(reached, a, b), new, before)

    return lax.fori_loop(0, length, hop, start)


def block_step(state, pieces):
    queries_b, keys_b, values_b, decay_b = pieces
    cumulative_memory = jnp.cumsum(decay_b, axis=0)
    total = cumulative_memory[-1]
    carried = jnp.exp(cumulative_memory)[:, :, None] * jnp.einsum(
        "thd,hde->the", queries_b.astype(jnp.float32), state, precision=HIGH
    )
    scores = jnp.einsum("thd,shd->hts", queries_b, keys_b, preferred_element_type=jnp.float32)
    length = cumulative_memory.shape[0]
    lower = jnp.tril(jnp.ones((length, length), dtype=bool))[None]
    spread = cumulative_memory.T[:, :, None] - cumulative_memory.T[:, None, :]
    weights = jnp.where(lower, jnp.exp(jnp.where(lower, spread, 0.0)), 0.0)
    mixes = (scores * weights).astype(jnp.bfloat16)
    local = jnp.einsum("hts,she->the", mixes, values_b, preferred_element_type=jnp.float32)
    scaled = keys_b.astype(jnp.float32) * jnp.exp(total[None, :] - cumulative_memory)[:, :, None]
    new_state = jnp.exp(total)[:, None, None] * state + jnp.einsum(
        "shd,she->hde", scaled, values_b.astype(jnp.float32), precision=HIGH
    )
    return (new_state, carried + local)


def normalize(attended, norm_gain, gate_logits):
    mean_square = jnp.mean(attended * attended, axis=-1, keepdims=True)
    normalized_output = attended * lax.rsqrt(mean_square + 1e-05)
    flat = normalized_output.reshape(attended.shape[0], -1)
    gated = flat * norm_gain[None, :] * jax.nn.sigmoid(gate_logits.astype(jnp.float32))
    return gated.astype(jnp.bfloat16)


def chain_link(earlier, later):
    return (earlier[0] * later[0], later[0][:, None, None] * earlier[1] + later[1])


def per_device(
    queries, key_vectors, value_rows, gate_logits, log_decay, initial_state, norm_gain, out_weight
):
    rows_here = queries.shape[0]
    head_count = log_decay.shape[1]
    head_dim = initial_state.shape[1]
    block_len = min(512, rows_here)
    block_count = rows_here // block_len

    def shaped(array):
        return array.reshape(block_count, block_len, head_count, head_dim)

    zero_state = jnp.zeros((head_count, head_dim, head_dim), jnp.float32)
    decay_blocks = log_decay.reshape(block_count, block_len, head_count)
    device_state, outputs = lax.scan(
        block_step,
        zero_state,
        (shaped(queries), shaped(key_vectors), shaped(value_rows), decay_blocks),
    )
    local_out = outputs.reshape(rows_here, head_count, head_dim)
    through = jnp.cumsum(log_decay, axis=0)
    shard_fading_rates = jnp.exp(through[-1])
    prior_decay, prior_state = entering(
        (shard_fading_rates, device_state),
        "seq",
        chain_link,
        (jnp.ones_like(shard_fading_rates), jnp.zeros_like(device_state)),
    )
    incoming = prior_decay[:, None, None] * initial_state + prior_state
    query_float = queries.reshape(rows_here, head_count, head_dim).astype(jnp.float32)
    inherited = jnp.exp(through)[:, :, None] * jnp.einsum(
        "thd,hde->the", query_float, incoming, precision=HIGH
    )
    attended = local_out + inherited
    hidden = normalize(attended, norm_gain, gate_logits)
    terms = jnp.dot(
        hidden,
        lax.all_gather(out_weight, "seq", axis=1, tiled=True),
        preferred_element_type=jnp.float32,
    )
    mixed = lax.psum_scatter(terms, "tensor", scatter_dimension=1, tiled=True)
    return mixed


def solution(mesh):
    return jax.shard_map(
        per_device,
        mesh=mesh,
        in_specs=(
            P("seq", "tensor"),
            P("seq", "tensor"),
            P("seq", "tensor"),
            P("seq", "tensor"),
            P("seq", "tensor"),
            P("tensor", None, None),
            P("tensor"),
            P("tensor", "seq"),
        ),
        out_specs=P("seq", "tensor"),
        check_vma=False,
    )
```

profile of v0, /device:TPU:4, one launch (start us, length us, event | category | flops | bytes accessed | tf_op | source)
XLA Modules:
  0.0 225.5 jit_solution(6239512811538646669)
XLA Ops:
  8.9 2.2 convolution_add_fusion
  12.0 21.1 %all-gather.1 = f32[32,1,8]{2,1,0:T(1,128)S(1)} all-gather(f32[1,1,8]{2,1,0:T(1,128)S(1)} %get-tuple-element.176), channel_id=1, replica_groups=mesh['seq'=32,'tensor'=8] {'seq'}, dimensions={0}, use_global_device_ids=true | all-gather | bytes 1056 | tf_op jit(solution)/shard_map/all_gather | solution.py:11
  33.8 57.9 %all-gather.7.cloned.1.call-done = f32[256,128,128]{2,1,0:T(8,128)} async-done(((f32[8,128,128]{2,1,0:T(8,128)}), f32[256,128,128]{2,1,0:T(8,128)}) %all-gather.7.cloned.1.call-update) | async-done | bytes 16777232 | tf_op jit(solution)/shard_map/all_gather | solution.py:11
  91.7 39.1 %while.10 = (s32[]{:T(128)}, f32[8]{0:T(128)S(1)}, f32[8,128,128]{2,1,0:T(8,128)S(1)}, s32[]{:T(128)}, f32[32,8]{1,0:T(8,128)S(1)}, /*index=5*/f32[32,8,128,128]{3,2,1,0:T(8,128)}, s32[]{:T(128)}, s32[]{:T(128)}) while((s32[]{:T(128)}, f32[8]{0:T(128)S(1)}, f32[8,128,128]{2,1,0:T(8,128)S(1)}, s32[]{:T(128)}, ...), condition=%wide.region_2.3_spmd.clone, body=%wide.region_1.2_spmd.clone.sunk | while | flops 524316 | bytes 1573139 | solution.py:23
  95.4 1.2 fusion.50
  96.6 1.2 fusion.50
  99.0 1.2 fusion.50
  100.2 1.2 fusion.50
  102.7 1.2 fusion.50
  103.9 1.2 fusion.50
  105.1 1.2 fusion.50
  106.4 1.2 fusion.50
  107.6 1.2 fusion.50
  110.0 1.2 fusion.50
  111.3 1.2 fusion.50
  112.5 1.2 fusion.50
  113.7 1.2 fusion.50
  114.9 1.2 fusion.50
  116.2 1.2 fusion.50
  119.9 1.2 fusion.50
  130.8 1.9 fusion.4
  133.5 28.2 %all-gather.5.cloned.1.call-done = bf16[1024,6144]{0,1:T(8,128)(2,1)} async-done(((bf16[1024,192]{0,1:T(8,128)(2,1)}), bf16[1024,6144]{0,1:T(8,128)(2,1)}) %all-gather.5.cloned.1.call-update) | async-done | bytes 12582928 | tf_op jit(solution)/shard_map/all_gather | solution.py:96
  161.7 10.4 %fusion.14 = f32[128,6144]{1,0:T(8,128)} fusion(bf16[1024,6144]{0,1:T(8,128)(2,1)} %all-gather.5.cloned.1.call-done, bf16[128,1024]{1,0:T(8,128)(2,1)S(1)} %copy-done.2, f32[128,1024]{1,0:T(8,128)S(1)} %copy.34, f32[1024]{0:T(1024)S(1)} %copy-done.3), kind=kOutput, calls=%fused_computation.25 | convolution fusion | flops 1611530240 | bytes 16519168 | tf_op jit(solution)/shard_map/dot_general | solution.py:94
  172.1 46.9 %reduce-scatter.2.cloned.1.call-done = f32[128,768]{1,0:T(8,128)} async-done(((f32[128,6144]{1,0:T(8,128)}), f32[128,768]{1,0:T(8,128)}) %reduce-scatter.2.cloned.1.call-update) | async-done | bytes 393232 | tf_op jit(solution)/shard_map/reduce_scatter | solution.py:99
  (79 shorter events, 24.0 us)
Async XLA Ops:
  6.5 26.6 %copy-start = (bf16[128,1024]{1,0:T(8,128)(2,1)S(1)}, bf16[128,1024]{1,0:T(8,128)(2,1)}, u32[]{:S(2)}) copy-start(bf16[128,1024]{1,0:T(8,128)(2,1)} %param.10) | copy-start | bytes 786436
  6.5 126.1 %copy-start.1 = (bf16[128,1024]{1,0:T(8,128)(2,1)S(1)}, bf16[128,1024]{1,0:T(8,128)(2,1)}, u32[]{:S(2)}) copy-start(bf16[128,1024]{1,0:T(8,128)(2,1)} %param.12) | copy-start | bytes 786436
  6.5 155.1 %copy-start.2 = (bf16[128,1024]{1,0:T(8,128)(2,1)S(1)}, bf16[128,1024]{1,0:T(8,128)(2,1)}, u32[]{:S(2)}) copy-start(bf16[128,1024]{1,0:T(8,128)(2,1)} %param.13) | copy-start | bytes 786436
  6.5 155.1 %copy-start.3 = (f32[1024]{0:T(1024)S(1)}, f32[1024]{0:T(1024)}, u32[]{:S(2)}) copy-start(f32[1024]{0:T(1024)} %param.16) | copy-start | bytes 12292
  6.5 85.1 %all-gather.7.cloned.1.call-start = ((), (), s32[]{:S(2)}) async-start(), calls=%async_computation.3 | async-start | bytes 17301504 | tf_op jit(solution)/shard_map/all_gather | solution.py:11
  11.1 150.6 %all-gather.5.cloned.1.call-start = ((), (), s32[]{:S(2)}) async-start(), calls=%async_computation.1 | async-start | bytes 12976128 | tf_op jit(solution)/shard_map/all_gather | solution.py:96
  11.8 207.2 %reduce-scatter.2.cloned.1.call-start = ((), (), s32[]{:S(2)}) async-start(), calls=%async_computation.2 | async-start | bytes 3538944 | tf_op jit(solution)/shard_map/reduce_scatter | solution.py:99
Sparse Core Ops, SparseCore 0:
  11.2 80.4 all-gather.6
  94.2 67.3 all-gather.4
  172.2 46.7 reduce-scatter.1
where the time goes:
time: 227 us; the launch traced here: 226 us
  waiting for transfers between devices  134 us (59%)
  other arithmetic  38.5 us (17%)
  blocking collectives  21.1 us (9%)
  matrix products  15.6 us (7%)
  between operations  13.2 us (6%)
  local copies, waits for them, and re-layouts  2.37 us (1%)
    all_gather x1, waiting for transfers between devices, entering(): everything = jax.tree.map(lambda part: lax.all_gather(part, axis), array)  57.9 us
    reduce_scatter x1, waiting for transfers between devices, per_device(): mixed = lax.psum_scatter(terms, 'tensor', scatter_dimension=1, tiled=True)  46.9 us
    select_n x64, other arithmetic, hop(): return jax.tree.map(lambda a, b: jnp.where(reached, a, b), new, before)  38.3 us
    all_gather x1, waiting for transfers between devices, per_device(): lax.all_gather(out_weight, 'seq', axis=1, tiled=True)  28.2 us
    all_gather x1, blocking collectives, entering(): everything = jax.tree.map(lambda part: lax.all_gather(part, axis), array)  21.1 us
    dot_general x1, matrix products, per_device(): jnp.dot(hidden, lax.all_gather(out_weight, 'seq', axis=1, tiled=True), pr...  10.4 us
  transfers between devices with their start and end apart: 3, of which 3 were waited for; matrix products, arithmetic and copies ran while one was open for 18% of the time, Pallas kernels for 0%

commit v1 on v0

--- a/solution.py
+++ b/solution.py
@@ -56,6 +56,35 @@
     return (earlier[0] * later[0], later[0][:, None, None] * earlier[1] + later[1])
 
 
+def pack(rates, state):
+    heads = state.shape[0]
+    flat = state.reshape(heads, -1)
+    lanes = jnp.broadcast_to(rates[:, None], (heads, 128))
+    return jnp.concatenate([flat, lanes], axis=1)
+
+
+def link_packed(earlier, later):
+    width = later.shape[1] - 128
+    later_rate = later[:, width:width + 1]
+    state = later_rate * earlier[:, :width] + later[:, :width]
+    rate = earlier[:, width:] * later[:, width:]
+    return jnp.concatenate([state, rate], axis=1)
+
+
+def carried_in(rates, state, initial_state):
+    length, mine = (lax.axis_size("seq"), lax.axis_index("seq"))
+    own = pack(rates, state)
+    shifted = lax.ppermute(own, "seq", [(i, i + 1) for i in range(length - 1)])
+    first = pack(jnp.ones_like(rates), initial_state)
+    current = jnp.where(mine == 0, first, shifted)
+    step = 1
+    while step < length:
+        earlier = lax.ppermute(current, "seq", [(i, i + step) for i in range(length - step)])
+        current = jnp.where(mine >= step, link_packed(earlier, current), current)
+        step *= 2
+    width = current.shape[1] - 128
+    return current[:, :width].reshape(state.shape)
+
 def per_device(
     queries, key_vectors, value_rows, gate_logits, log_decay, initial_state, norm_gain, out_weight
 ):
@@ -78,13 +107,7 @@
     local_out = outputs.reshape(rows_here, head_count, head_dim)
     through = jnp.cumsum(log_decay, axis=0)
     shard_fading_rates = jnp.exp(through[-1])
-    prior_decay, prior_state = entering(
-        (shard_fading_rates, device_state),
-        "seq",
-        chain_link,
-        (jnp.ones_like(shard_fading_rates), jnp.zeros_like(device_state)),
-    )
-    incoming = prior_decay[:, None, None] * initial_state + prior_state
+    incoming = carried_in(shard_fading_rates, device_state, initial_state)
     query_float = queries.reshape(rows_here, head_count, head_dim).astype(jnp.float32)
     inherited = jnp.exp(through)[:, :, None] * jnp.einsum(
         "thd,hde->the", query_float, incoming, precision=HIGH

time: 227 us -> 194 us (0.85)
  other arithmetic: 38.5 us -> 1.34 us
  starting transfers between devices: 0.11 us -> 22.3 us
  blocking collectives: 21.1 us -> 0 us
  waiting for transfers between devices: 134 us -> 138 us
  local copies, waits for them, and re-layouts: 2.37 us -> 4.69 us
    ppermute x0 -> x6, waiting for transfers between devices: none -> 81.1 us  [the longest x5 73.9 us: carried_in(): lax.ppermute(current, 'seq', [(i, i + step) for i in range(length - step)])]
    all_gather x1 -> x0, waiting for transfers between devices: 57.9 us -> none  [entering(): everything = jax.tree.map(lambda part: lax.all_gather(part, axis), array)]
    select_n x64 -> x5, other arithmetic: 38.3 us -> 0.3 us  [the longest x4 0.23 us: carried_in(): current = jnp.where(mine >= step, link_packed(earlier, current), current)]
    all_gather x1, waiting for transfers between devices: 28.2 us -> 4.19 us  [per_device(): lax.all_gather(out_weight, 'seq', axis=1, tiled=True)]
    ppermute x0 -> x6, starting transfers between devices: none -> 22.3 us  [the longest x5 20.4 us: carried_in(): lax.ppermute(current, 'seq', [(i, i + step) for i in range(length - step)])]
    all_gather x1 -> x0, blocking collectives: 21.1 us -> none  [entering(): everything = jax.tree.map(lambda part: lax.all_gather(part, axis), array)]
    reduce_scatter x1, waiting for transfers between devices: 46.9 us -> 52.9 us  [per_device(): mixed = lax.psum_scatter(terms, 'tensor', scatter_dimension=1, tiled=True)]
  transfers between devices with their start and end apart: 3 -> 8, of which waited for: 3 -> 8; matrix products, arithmetic and copies ran while one was open for 18% -> 3% of each run, Pallas kernels for 0% -> 0%
where the time goes in v1:
time: 194 us
  waiting for transfers between devices  138 us (71%)
  starting transfers between devices  22.3 us (11%)
  between operations  13.7 us (7%)
  matrix products  13.6 us (7%)
  local copies, waits for them, and re-layouts  4.69 us (2%)
    ppermute x5, waiting for transfers between devices, carried_in(): lax.ppermute(current, 'seq', [(i, i + step) for i in range(length - step)])  73.9 us
    reduce_scatter x1, waiting for transfers between devices, per_device(): mixed = lax.psum_scatter(terms, 'tensor', scatter_dimension=1, tiled=True)  52.9 us
    ppermute x5, starting transfers between devices, carried_in(): lax.ppermute(current, 'seq', [(i, i + step) for i in range(length - step)])  20.4 us
    dot_general x1, matrix products, per_device(): jnp.dot(hidden, lax.all_gather(out_weight, 'seq', axis=1, tiled=True), pr...  10.4 us
    ppermute x1, waiting for transfers between devices, carried_in(): shifted = lax.ppermute(own, 'seq', [(i, i + 1) for i in range(length - 1)])  7.19 us
    all_gather x1, waiting for transfers between devices, per_device(): lax.all_gather(out_weight, 'seq', axis=1, tiled=True)  4.19 us
  transfers between devices with their start and end apart: 8, of which 8 were waited for; matrix products, arithmetic and copies ran while one was open for 3% of the time, Pallas kernels for 0%

profile of v1, /device:TPU:4, one launch (start us, length us, event | category | flops | bytes accessed | tf_op | source)
XLA Modules:
  0.0 193.9 jit_solution(17342505612734272068)
XLA Ops:
  6.5 0.8 copy.36
  7.7 1.1 copy.53
  8.8 1.4 fusion.4
  10.2 0.3 copy.90
  10.6 1.9 collective-permute-start
  12.5 1.4 copy.91
  13.9 7.2 %collective-permute-done = f32[8,16512]{1,0:T(8,128)S(1)} collective-permute-done((f32[8,16512]{1,0:T(8,128)S(1)}, f32[8,16512]{1,0:T(8,128)S(1)}, u32[]{:S(2)}, u32[]{:S(2)}) %collective-permute-start) | collective-permute-done | bytes 528416 | tf_op jit(solution)/shard_map/ppermute | solution.py:77
  21.2 1.9 collective-permute-start.1
  23.3 8.5 %collective-permute-done.1 = f32[8,16512]{1,0:T(8,128)S(1)} collective-permute-done((f32[8,16512]{1,0:T(8,128)S(1)}, f32[8,16512]{1,0:T(8,128)S(1)}, u32[]{:S(2)}, u32[]{:S(2)}) %collective-permute-start.1) | collective-permute-done | bytes 528416 | tf_op jit(solution)/shard_map/ppermute | solution.py:82
  32.0 3.1 %collective-permute-start.2 = (f32[8,16512]{1,0:T(8,128)S(1)}, f32[8,16512]{1,0:T(8,128)S(1)}, u32[]{:S(2)}, u32[]{:S(2)}) collective-permute-start(f32[8,16512]{1,0:T(8,128)S(1)} %maximum_select_fusion), channel_id=1, source_target_pairs={{0,16},{8,24},{16,32},{24,40},{32,48},{40,56},{48,64},{56,72},{64,... | collective-permute-start | bytes 1585160 | tf_op jit(solution)/shard_map/ppermute | solution.py:82
  35.3 11.9 %collective-permute-done.2 = f32[8,16512]{1,0:T(8,128)S(1)} collective-permute-done((f32[8,16512]{1,0:T(8,128)S(1)}, f32[8,16512]{1,0:T(8,128)S(1)}, u32[]{:S(2)}, u32[]{:S(2)}) %collective-permute-start.2) | collective-permute-done | bytes 528416 | tf_op jit(solution)/shard_map/ppermute | solution.py:82
  47.4 6.2 %collective-permute-start.3 = (f32[8,16512]{1,0:T(8,128)S(1)}, f32[8,16512]{1,0:T(8,128)S(1)}, u32[]{:S(2)}, u32[]{:S(2)}) collective-permute-start(f32[8,16512]{1,0:T(8,128)S(1)} %maximum_select_fusion.1), channel_id=1, source_target_pairs={{0,32},{8,40},{16,48},{24,56},{32,64},{40,72},{48,80},{56,88},{64,... | collective-permute-start | bytes 1585160 | tf_op jit(solution)/shard_map/ppermute | solution.py:82
  53.7 17.7 %collective-permute-done.3 = f32[8,16512]{1,0:T(8,128)S(1)} collective-permute-done((f32[8,16512]{1,0:T(8,128)S(1)}, f32[8,16512]{1,0:T(8,128)S(1)}, u32[]{:S(2)}, u32[]{:S(2)}) %collective-permute-start.3) | collective-permute-done | bytes 528416 | tf_op jit(solution)/shard_map/ppermute | solution.py:82
  71.6 3.5 %collective-permute-start.4 = (f32[8,16512]{1,0:T(8,128)S(1)}, f32[8,16512]{1,0:T(8,128)S(1)}, u32[]{:S(2)}, u32[]{:S(2)}) collective-permute-start(f32[8,16512]{1,0:T(8,128)S(1)} %maximum_select_fusion.2), channel_id=1, source_target_pairs={{0,64},{8,72},{16,80},{24,88},{32,96},{40,104},{48,112},{56,120},{... | collective-permute-start | bytes 1585160 | tf_op jit(solution)/shard_map/ppermute | solution.py:82
  75.2 15.0 %collective-permute-done.4 = f32[8,16512]{1,0:T(8,128)S(1)} collective-permute-done((f32[8,16512]{1,0:T(8,128)S(1)}, f32[8,16512]{1,0:T(8,128)S(1)}, u32[]{:S(2)}, u32[]{:S(2)}) %collective-permute-start.4) | collective-permute-done | bytes 528416 | tf_op jit(solution)/shard_map/ppermute | solution.py:82
  90.4 5.7 %collective-permute-start.5 = (f32[8,16512]{1,0:T(8,128)S(1)}, f32[8,16512]{1,0:T(8,128)S(1)}, u32[]{:S(2)}, u32[]{:S(2)}) collective-permute-start(f32[8,16512]{1,0:T(8,128)S(1)} %maximum_select_fusion.3), channel_id=1, source_target_pairs={{0,128},{8,136},{16,144},{24,152},{32,160},{40,168},{48,176},{56,1... | collective-permute-start | bytes 1585160 | tf_op jit(solution)/shard_map/ppermute | solution.py:82
  96.3 0.7 fusion.2
  97.1 20.7 %collective-permute-done.5 = f32[8,16512]{1,0:T(8,128)S(1)} collective-permute-done((f32[8,16512]{1,0:T(8,128)S(1)}, f32[8,16512]{1,0:T(8,128)S(1)}, u32[]{:S(2)}, u32[]{:S(2)}) %collective-permute-start.5) | collective-permute-done | bytes 528416 | tf_op jit(solution)/shard_map/ppermute | solution.py:82
  118.0 0.6 fusion.3
  118.6 0.5 multiply_reduce_fusion
  119.2 0.2 copy.50
  119.4 4.2 %all-gather.2.cloned.1.call-done = bf16[1024,6144]{0,1:T(8,128)(2,1)} async-done(((bf16[1024,192]{0,1:T(8,128)(2,1)}), bf16[1024,6144]{0,1:T(8,128)(2,1)}) %all-gather.2.cloned.1.call-update) | async-done | bytes 12582928 | tf_op jit(solution)/shard_map/all_gather | solution.py:119
  123.6 10.4 %fusion.17 = f32[128,6144]{1,0:T(8,128)} fusion(bf16[1024,6144]{0,1:T(8,128)(2,1)} %all-gather.2.cloned.1.call-done, bf16[128,1024]{1,0:T(8,128)(2,1)S(1)} %copy-done.2, f32[128,1024]{1,0:T(8,128)S(1)} %copy.50, f32[1024]{0:T(1024)S(1)} %copy-done.3), kind=kOutput, calls=%fused_computation.42 | convolution fusion | flops 1611530240 | bytes 16519168 | tf_op jit(solution)/shard_map/dot_general | solution.py:117
  134.1 52.9 %reduce-scatter.2.cloned.1.call-done = f32[128,768]{1,0:T(8,128)} async-done(((f32[128,6144]{1,0:T(8,128)}), f32[128,768]{1,0:T(8,128)}) %reduce-scatter.2.cloned.1.call-update) | async-done | bytes 393232 | tf_op jit(solution)/shard_map/reduce_scatter | solution.py:122
  (45 shorter events, 2.2 us)
Async XLA Ops:
  6.5 89.8 %copy-start = (bf16[128,1024]{1,0:T(8,128)(2,1)S(1)}, bf16[128,1024]{1,0:T(8,128)(2,1)}, u32[]{:S(2)}) copy-start(bf16[128,1024]{1,0:T(8,128)(2,1)} %param.8) | copy-start | bytes 786436
  6.5 117.1 %all-gather.2.cloned.1.call-start = ((), (), s32[]{:S(2)}) async-start(), calls=%async_computation.1 | async-start | bytes 12976128 | tf_op jit(solution)/shard_map/all_gather | solution.py:119
  7.5 111.1 %copy-start.1 = (bf16[128,1024]{1,0:T(8,128)(2,1)S(1)}, bf16[128,1024]{1,0:T(8,128)(2,1)}, u32[]{:S(2)}) copy-start(bf16[128,1024]{1,0:T(8,128)(2,1)} %param.10) | copy-start | bytes 786436
  10.6 10.5 %collective-permute-start = (f32[8,16512]{1,0:T(8,128)S(1)}, f32[8,16512]{1,0:T(8,128)S(1)}, u32[]{:S(2)}, u32[]{:S(2)}) collective-permute-start(f32[8,16512]{1,0:T(8,128)S(1)} %pad_maximum_fusion), channel_id=1, source_target_pairs={{0,8},{8,16},{16,24},{24,32},{32,40},{40,48},{48,56},{56,64},{64,7... | collective-permute-start | bytes 1585160 | tf_op jit(solution)/shard_map/ppermute | solution.py:77
  12.5 111.1 %copy-start.2 = (bf16[128,1024]{1,0:T(8,128)(2,1)S(1)}, bf16[128,1024]{1,0:T(8,128)(2,1)}, u32[]{:S(2)}) copy-start(bf16[128,1024]{1,0:T(8,128)(2,1)} %param.11) | copy-start | bytes 786436
  12.5 111.1 %copy-start.3 = (f32[1024]{0:T(1024)S(1)}, f32[1024]{0:T(1024)}, u32[]{:S(2)}) copy-start(f32[1024]{0:T(1024)} %param.14) | copy-start | bytes 12292
  21.2 10.5 %collective-permute-start.1 = (f32[8,16512]{1,0:T(8,128)S(1)}, f32[8,16512]{1,0:T(8,128)S(1)}, u32[]{:S(2)}, u32[]{:S(2)}) collective-permute-start(f32[8,16512]{1,0:T(8,128)S(1)} %pad_select_fusion), channel_id=1, source_target_pairs={{0,8},{8,16},{16,24},{24,32},{32,40},{40,48},{48,56},{56,64},{64,7... | collective-permute-start | bytes 1585160 | tf_op jit(solution)/shard_map/ppermute | solution.py:82
  32.0 15.2 %collective-permute-start.2 = (f32[8,16512]{1,0:T(8,128)S(1)}, f32[8,16512]{1,0:T(8,128)S(1)}, u32[]{:S(2)}, u32[]{:S(2)}) collective-permute-start(f32[8,16512]{1,0:T(8,128)S(1)} %maximum_select_fusion), channel_id=1, source_target_pairs={{0,16},{8,24},{16,32},{24,40},{32,48},{40,56},{48,64},{56,72},{64,... | collective-permute-start | bytes 1585160 | tf_op jit(solution)/shard_map/ppermute | solution.py:82
  35.1 151.9 %reduce-scatter.2.cloned.1.call-start = ((), (), s32[]{:S(2)}) async-start(), calls=%async_computation.2 | async-start | bytes 3538944 | tf_op jit(solution)/shard_map/reduce_scatter | solution.py:122
  47.4 24.0 %collective-permute-start.3 = (f32[8,16512]{1,0:T(8,128)S(1)}, f32[8,16512]{1,0:T(8,128)S(1)}, u32[]{:S(2)}, u32[]{:S(2)}) collective-permute-start(f32[8,16512]{1,0:T(8,128)S(1)} %maximum_select_fusion.1), channel_id=1, source_target_pairs={{0,32},{8,40},{16,48},{24,56},{32,64},{40,72},{48,80},{56,88},{64,... | collective-permute-start | bytes 1585160 | tf_op jit(solution)/shard_map/ppermute | solution.py:82
  71.6 18.6 %collective-permute-start.4 = (f32[8,16512]{1,0:T(8,128)S(1)}, f32[8,16512]{1,0:T(8,128)S(1)}, u32[]{:S(2)}, u32[]{:S(2)}) collective-permute-start(f32[8,16512]{1,0:T(8,128)S(1)} %maximum_select_fusion.2), channel_id=1, source_target_pairs={{0,64},{8,72},{16,80},{24,88},{32,96},{40,104},{48,112},{56,120},{... | collective-permute-start | bytes 1585160 | tf_op jit(solution)/shard_map/ppermute | solution.py:82
  90.4 27.4 %collective-permute-start.5 = (f32[8,16512]{1,0:T(8,128)S(1)}, f32[8,16512]{1,0:T(8,128)S(1)}, u32[]{:S(2)}, u32[]{:S(2)}) collective-permute-start(f32[8,16512]{1,0:T(8,128)S(1)} %maximum_select_fusion.3), channel_id=1, source_target_pairs={{0,128},{8,136},{16,144},{24,152},{32,160},{40,168},{48,176},{56,1... | collective-permute-start | bytes 1585160 | tf_op jit(solution)/shard_map/ppermute | solution.py:82
Sparse Core Ops, SparseCore 0:
  35.2 88.3 all-gather.1
  134.2 52.7 reduce-scatter.1

commit v2 on v1

--- a/solution.py
+++ b/solution.py
@@ -114,12 +114,19 @@
     )
     attended = local_out + inherited
     hidden = normalize(attended, norm_gain, gate_logits)
-    terms = jnp.dot(
-        hidden,
-        lax.all_gather(out_weight, "seq", axis=1, tiled=True),
-        preferred_element_type=jnp.float32,
-    )
-    mixed = lax.psum_scatter(terms, "tensor", scatter_dimension=1, tiled=True)
+    seq_len, tensor_len = (lax.axis_size("seq"), lax.axis_size("tensor"))
+    col_blocks = seq_len // tensor_len
+    route = []
+    for s in range(seq_len):
+        for t in range(tensor_len):
+            source = (col_blocks * t + s // tensor_len) * tensor_len + s % tensor_len
+            route.append((source, s * tensor_len + t))
+    placed = lax.ppermute(out_weight, ("seq", "tensor"), route)
+    columns = lax.all_gather(placed, "seq", axis=0, tiled=True)
+    columns = columns.reshape(col_blocks, -1, columns.shape[1])
+    full_hidden = lax.all_gather(hidden, "tensor", axis=1, tiled=True)
+    mixed = jnp.einsum("tk,rkc->trc", full_hidden, columns, preferred_element_type=jnp.float32)
+    mixed = mixed.reshape(rows_here, -1)
     return mixed
 
 

time: 194 us -> 231 us (1.19)
  local copies, waits for them, and re-layouts: 4.69 us -> 41.3 us
    reduce_scatter x1 -> x0, waiting for transfers between devices: 52.9 us -> none  [per_device(): mixed = lax.psum_scatter(terms, 'tensor', scatter_dimension=1, tiled=True)]
    all_gather x1 -> x2, waiting for transfers between devices: 4.19 us -> 46.6 us  [the longest x1 40 us: per_device(): columns = lax.all_gather(placed, 'seq', axis=0, tiled=True)]
    ppermute x0 -> x1, waiting for transfers between devices: none -> 25.3 us  [per_device(): placed = lax.ppermute(out_weight, ('seq', 'tensor'), route)]
    reshape x0 -> x1, local copies, waits for them, and re-layouts: none -> 21.3 us  [per_device(): columns = columns.reshape(col_blocks, -1, columns.shape[1])]
    dot_general x0 -> x1, local copies, waits for them, and re-layouts: none -> 14.5 us  [per_device(): jnp.einsum('tk,rkc->trc', full_hidden, columns, preferred_element_type=jn...]
    ppermute x5, waiting for transfers between devices: 73.9 us -> 60.1 us  [carried_in(): lax.ppermute(current, 'seq', [(i, i + step) for i in range(length - step)])]
    ppermute x5, starting transfers between devices: 20.4 us -> 14.1 us  [carried_in(): lax.ppermute(current, 'seq', [(i, i + step) for i in range(length - step)])]
    ppermute x0 -> x1, starting transfers between devices: none -> 4.09 us  [per_device(): placed = lax.ppermute(out_weight, ('seq', 'tensor'), route)]
  transfers between devices with their start and end apart: 8 -> 9, of which waited for: 8 -> 9; matrix products, arithmetic and copies ran while one was open for 3% -> 18% of each run, Pallas kernels for 0% -> 0%
where the time goes in v2:
time: 231 us; the launch traced here: 230 us
  waiting for transfers between devices  139 us (60%)
  local copies, waits for them, and re-layouts  41.3 us (18%)
  starting transfers between devices  20.1 us (9%)
  between operations  13.7 us (6%)
  matrix products  13.4 us (6%)
    ppermute x5, waiting for transfers between devices, carried_in(): lax.ppermute(current, 'seq', [(i, i + step) for i in range(length - step)])  60.1 us
    all_gather x1, waiting for transfers between devices, per_device(): columns = lax.all_gather(placed, 'seq', axis=0, tiled=True)  40 us
    ppermute x1, waiting for transfers between devices, per_device(): placed = lax.ppermute(out_weight, ('seq', 'tensor'), route)  25.3 us
    reshape x1, local copies, waits for them, and re-layouts, per_device(): columns = columns.reshape(col_blocks, -1, columns.shape[1])  21.3 us
    dot_general x1, local copies, waits for them, and re-layouts, per_device(): jnp.einsum('tk,rkc->trc', full_hidden, columns, preferred_element_type=jn...  14.5 us
    ppermute x5, starting transfers between devices, carried_in(): lax.ppermute(current, 'seq', [(i, i + step) for i in range(length - step)])  14.1 us
    dot_general x1, matrix products, per_device(): jnp.einsum('tk,rkc->trc', full_hidden, columns, preferred_element_type=jn...  10.2 us
    ppermute x1, waiting for transfers between devices, carried_in(): shifted = lax.ppermute(own, 'seq', [(i, i + 1) for i in range(length - 1)])  7.19 us
  transfers between devices with their start and end apart: 9, of which 9 were waited for; matrix products, arithmetic and copies ran while one was open for 18% of the time, Pallas kernels for 0%

profile of v2, /device:TPU:4, one launch (start us, length us, event | category | flops | bytes accessed | tf_op | source)
XLA Modules:
  0.0 229.9 jit_solution(4857555923900355773)
XLA Ops:
  6.5 0.8 copy.36
  7.7 1.1 copy.54
  8.8 1.4 fusion.4
  10.6 1.9 collective-permute-start
  12.5 1.4 copy.92
  13.9 7.2 %collective-permute-done = f32[8,16512]{1,0:T(8,128)S(1)} collective-permute-done((f32[8,16512]{1,0:T(8,128)S(1)}, f32[8,16512]{1,0:T(8,128)S(1)}, u32[]{:S(2)}, u32[]{:S(2)}) %collective-permute-start) | collective-permute-done | bytes 528416 | tf_op jit(solution)/shard_map/ppermute | solution.py:77
  21.2 1.9 collective-permute-start.1
  23.2 8.5 %collective-permute-done.1 = f32[8,16512]{1,0:T(8,128)S(1)} collective-permute-done((f32[8,16512]{1,0:T(8,128)S(1)}, f32[8,16512]{1,0:T(8,128)S(1)}, u32[]{:S(2)}, u32[]{:S(2)}) %collective-permute-start.1) | collective-permute-done | bytes 528416 | tf_op jit(solution)/shard_map/ppermute | solution.py:82
  32.0 3.1 %collective-permute-start.2 = (f32[8,16512]{1,0:T(8,128)S(1)}, f32[8,16512]{1,0:T(8,128)S(1)}, u32[]{:S(2)}, u32[]{:S(2)}) collective-permute-start(f32[8,16512]{1,0:T(8,128)S(1)} %maximum_select_fusion), channel_id=1, source_target_pairs={{0,16},{8,24},{16,32},{24,40},{32,48},{40,56},{48,64},{56,72},{64,... | collective-permute-start | bytes 1585160 | tf_op jit(solution)/shard_map/ppermute | solution.py:82
  35.1 4.1 %collective-permute-start.6 = (bf16[1024,192]{0,1:T(8,128)(2,1)}, bf16[1024,192]{0,1:T(8,128)(2,1)S(1)}, u32[]{:S(2)}, u32[]{:S(2)}) collective-permute-start(bf16[1024,192]{0,1:T(8,128)(2,1)} %param.15), channel_id=1, source_target_pairs={{0,0},{32,1},{64,2},{96,3},{128,4},{160,5},{192,6},{224,7},{1,8},{... | collective-permute-start | bytes 1179656 | tf_op jit(solution)/shard_map/ppermute | solution.py:124
  39.2 25.3 %collective-permute-done.6 = bf16[1024,192]{0,1:T(8,128)(2,1)S(1)} collective-permute-done((bf16[1024,192]{0,1:T(8,128)(2,1)}, bf16[1024,192]{0,1:T(8,128)(2,1)S(1)}, u32[]{:S(2)}, u32[]{:S(2)}) %collective-permute-start.6) | collective-permute-done | bytes 393248 | tf_op jit(solution)/shard_map/ppermute | solution.py:124
  65.4 14.9 %collective-permute-done.2 = f32[8,16512]{1,0:T(8,128)S(1)} collective-permute-done((f32[8,16512]{1,0:T(8,128)S(1)}, f32[8,16512]{1,0:T(8,128)S(1)}, u32[]{:S(2)}, u32[]{:S(2)}) %collective-permute-start.2) | collective-permute-done | bytes 528416 | tf_op jit(solution)/shard_map/ppermute | solution.py:82
  80.5 3.9 %collective-permute-start.3 = (f32[8,16512]{1,0:T(8,128)S(1)}, f32[8,16512]{1,0:T(8,128)S(1)}, u32[]{:S(2)}, u32[]{:S(2)}) collective-permute-start(f32[8,16512]{1,0:T(8,128)S(1)} %maximum_select_fusion.1), channel_id=1, source_target_pairs={{0,32},{8,40},{16,48},{24,56},{32,64},{40,72},{48,80},{56,88},{64,... | collective-permute-start | bytes 1585160 | tf_op jit(solution)/shard_map/ppermute | solution.py:82
  84.5 11.3 %collective-permute-done.3 = f32[8,16512]{1,0:T(8,128)S(1)} collective-permute-done((f32[8,16512]{1,0:T(8,128)S(1)}, f32[8,16512]{1,0:T(8,128)S(1)}, u32[]{:S(2)}, u32[]{:S(2)}) %collective-permute-start.3) | collective-permute-done | bytes 528416 | tf_op jit(solution)/shard_map/ppermute | solution.py:82
  96.0 2.4 %collective-permute-start.4 = (f32[8,16512]{1,0:T(8,128)S(1)}, f32[8,16512]{1,0:T(8,128)S(1)}, u32[]{:S(2)}, u32[]{:S(2)}) collective-permute-start(f32[8,16512]{1,0:T(8,128)S(1)} %maximum_select_fusion.2), channel_id=1, source_target_pairs={{0,64},{8,72},{16,80},{24,88},{32,96},{40,104},{48,112},{56,120},{... | collective-permute-start | bytes 1585160 | tf_op jit(solution)/shard_map/ppermute | solution.py:82
  98.5 15.4 %collective-permute-done.4 = f32[8,16512]{1,0:T(8,128)S(1)} collective-permute-done((f32[8,16512]{1,0:T(8,128)S(1)}, f32[8,16512]{1,0:T(8,128)S(1)}, u32[]{:S(2)}, u32[]{:S(2)}) %collective-permute-start.4) | collective-permute-done | bytes 528416 | tf_op jit(solution)/shard_map/ppermute | solution.py:82
  114.2 2.8 %collective-permute-start.5 = (f32[8,16512]{1,0:T(8,128)S(1)}, f32[8,16512]{1,0:T(8,128)S(1)}, u32[]{:S(2)}, u32[]{:S(2)}) collective-permute-start(f32[8,16512]{1,0:T(8,128)S(1)} %maximum_select_fusion.3), channel_id=1, source_target_pairs={{0,128},{8,136},{16,144},{24,152},{32,160},{40,168},{48,176},{56,1... | collective-permute-start | bytes 1585160 | tf_op jit(solution)/shard_map/ppermute | solution.py:82
  117.9 10.0 %collective-permute-done.5 = f32[8,16512]{1,0:T(8,128)S(1)} collective-permute-done((f32[8,16512]{1,0:T(8,128)S(1)}, f32[8,16512]{1,0:T(8,128)S(1)}, u32[]{:S(2)}, u32[]{:S(2)}) %collective-permute-start.5) | collective-permute-done | bytes 528416 | tf_op jit(solution)/shard_map/ppermute | solution.py:82
  129.5 0.9 multiply_convert_fusion
  130.4 40.0 %all-gather.5.cloned.1.call-done = bf16[32768,192]{0,1:T(8,128)(2,1)} async-done(((bf16[1024,192]{0,1:T(8,128)(2,1)}), bf16[32768,192]{0,1:T(8,128)(2,1)}) %all-gather.5.cloned.1.call-update) | async-done | bytes 12582928 | tf_op jit(solution)/shard_map/all_gather | solution.py:125
  170.4 21.3 %reshape.82 = bf16[4,8192,192]{1,0,2:T(4,128)(2,1)} reshape(bf16[32768,192]{0,1:T(8,128)(2,1)} %all-gather.5.cloned.1.call-done) | data formatting | bytes 25165824 | tf_op jit(solution)/shard_map/reshape | solution.py:126
  191.7 14.5 %copy.51 = bf16[4,192,8192]{2,1,0:T(8,128)(2,1)} copy(bf16[4,192,8192]{2,0,1:T(4,128)(2,1)} %bitcast.80) | data formatting | bytes 25165824 | tf_op jit(solution)/shard_map/tk,rkc->trc/dot_general | solution.py:128
  206.2 6.6 %all-gather.3.cloned.1.call-done = bf16[128,8192]{1,0:T(8,128)(2,1)} async-done(((bf16[128,1024]{1,0:T(8,128)(2,1)}), bf16[128,8192]{1,0:T(8,128)(2,1)}) %all-gather.3.cloned.1.call-update) | async-done | bytes 2097168 | tf_op jit(solution)/shard_map/all_gather | solution.py:127
  212.8 10.2 %fusion.41 = f32[128,768]{1,0:T(8,128)} fusion(bf16[128,8192]{1,0:T(8,128)(2,1)} %all-gather.3.cloned.1.call-done, bf16[768,8192]{1,0:T(8,128)(2,1)} %bitcast.79), kind=kOutput, calls=%fused_computation.78 | convolution fusion | flops 1610612736 | bytes 15073280 | tf_op jit(solution)/shard_map/tk,rkc->trc/dot_general | solution.py:128
  (52 shorter events, 5.3 us)
Async XLA Ops:
  6.5 110.6 %copy-start = (bf16[128,1024]{1,0:T(8,128)(2,1)S(1)}, bf16[128,1024]{1,0:T(8,128)(2,1)}, u32[]{:S(2)}) copy-start(bf16[128,1024]{1,0:T(8,128)(2,1)} %param.8) | copy-start | bytes 786436
  6.5 163.9 %all-gather.5.cloned.1.call-start = ((), (), s32[]{:S(2)}) async-start(), calls=%async_computation.1 | async-start | bytes 12976128 | tf_op jit(solution)/shard_map/all_gather | solution.py:125
  7.5 121.2 %copy-start.1 = (bf16[128,1024]{1,0:T(8,128)(2,1)S(1)}, bf16[128,1024]{1,0:T(8,128)(2,1)}, u32[]{:S(2)}) copy-start(bf16[128,1024]{1,0:T(8,128)(2,1)} %param.10) | copy-start | bytes 786436
  10.6 10.5 %collective-permute-start = (f32[8,16512]{1,0:T(8,128)S(1)}, f32[8,16512]{1,0:T(8,128)S(1)}, u32[]{:S(2)}, u32[]{:S(2)}) collective-permute-start(f32[8,16512]{1,0:T(8,128)S(1)} %pad_maximum_fusion), channel_id=1, source_target_pairs={{0,8},{8,16},{16,24},{24,32},{32,40},{40,48},{48,56},{56,64},{64,7... | collective-permute-start | bytes 1585160 | tf_op jit(solution)/shard_map/ppermute | solution.py:77
  12.5 117.0 %copy-start.3 = (bf16[128,1024]{1,0:T(8,128)(2,1)S(1)}, bf16[128,1024]{1,0:T(8,128)(2,1)}, u32[]{:S(2)}) copy-start(bf16[128,1024]{1,0:T(8,128)(2,1)} %param.11) | copy-start | bytes 786436
  12.5 117.0 %copy-start.4 = (f32[1024]{0:T(1024)S(1)}, f32[1024]{0:T(1024)}, u32[]{:S(2)}) copy-start(f32[1024]{0:T(1024)} %param.14) | copy-start | bytes 12292
  21.2 10.5 %collective-permute-start.1 = (f32[8,16512]{1,0:T(8,128)S(1)}, f32[8,16512]{1,0:T(8,128)S(1)}, u32[]{:S(2)}, u32[]{:S(2)}) collective-permute-start(f32[8,16512]{1,0:T(8,128)S(1)} %pad_select_fusion), channel_id=1, source_target_pairs={{0,8},{8,16},{16,24},{24,32},{32,40},{40,48},{48,56},{56,64},{64,7... | collective-permute-start | bytes 1585160 | tf_op jit(solution)/shard_map/ppermute | solution.py:82
  32.0 48.3 %collective-permute-start.2 = (f32[8,16512]{1,0:T(8,128)S(1)}, f32[8,16512]{1,0:T(8,128)S(1)}, u32[]{:S(2)}, u32[]{:S(2)}) collective-permute-start(f32[8,16512]{1,0:T(8,128)S(1)} %maximum_select_fusion), channel_id=1, source_target_pairs={{0,16},{8,24},{16,32},{24,40},{32,48},{40,56},{48,64},{56,72},{64,... | collective-permute-start | bytes 1585160 | tf_op jit(solution)/shard_map/ppermute | solution.py:82
  35.1 29.4 %collective-permute-start.6 = (bf16[1024,192]{0,1:T(8,128)(2,1)}, bf16[1024,192]{0,1:T(8,128)(2,1)S(1)}, u32[]{:S(2)}, u32[]{:S(2)}) collective-permute-start(bf16[1024,192]{0,1:T(8,128)(2,1)} %param.15), channel_id=1, source_target_pairs={{0,0},{32,1},{64,2},{96,3},{128,4},{160,5},{192,6},{224,7},{1,8},{... | collective-permute-start | bytes 1179656 | tf_op jit(solution)/shard_map/ppermute | solution.py:124
  64.5 0.7 copy-start.2
  65.3 147.5 %all-gather.3.cloned.1.call-start = ((), (), s32[]{:S(2)}) async-start(), calls=%async_computation | async-start | bytes 2359296 | tf_op jit(solution)/shard_map/all_gather | solution.py:127
  80.5 15.3 %collective-permute-start.3 = (f32[8,16512]{1,0:T(8,128)S(1)}, f32[8,16512]{1,0:T(8,128)S(1)}, u32[]{:S(2)}, u32[]{:S(2)}) collective-permute-start(f32[8,16512]{1,0:T(8,128)S(1)} %maximum_select_fusion.1), channel_id=1, source_target_pairs={{0,32},{8,40},{16,48},{24,56},{32,64},{40,72},{48,80},{56,88},{64,... | collective-permute-start | bytes 1585160 | tf_op jit(solution)/shard_map/ppermute | solution.py:82
  96.0 17.9 %collective-permute-start.4 = (f32[8,16512]{1,0:T(8,128)S(1)}, f32[8,16512]{1,0:T(8,128)S(1)}, u32[]{:S(2)}, u32[]{:S(2)}) collective-permute-start(f32[8,16512]{1,0:T(8,128)S(1)} %maximum_select_fusion.2), channel_id=1, source_target_pairs={{0,64},{8,72},{16,80},{24,88},{32,96},{40,104},{48,112},{56,120},{... | collective-permute-start | bytes 1585160 | tf_op jit(solution)/shard_map/ppermute | solution.py:82
  114.2 13.7 %collective-permute-start.5 = (f32[8,16512]{1,0:T(8,128)S(1)}, f32[8,16512]{1,0:T(8,128)S(1)}, u32[]{:S(2)}, u32[]{:S(2)}) collective-permute-start(f32[8,16512]{1,0:T(8,128)S(1)} %maximum_select_fusion.3), channel_id=1, source_target_pairs={{0,128},{8,136},{16,144},{24,152},{32,160},{40,168},{48,176},{56,1... | collective-permute-start | bytes 1585160 | tf_op jit(solution)/shard_map/ppermute | solution.py:82
Sparse Core Ops, SparseCore 0:
  65.4 104.9 all-gather.4
  172.2 40.5 all-gather.2

commit v3 on v1

--- a/solution.py
+++ b/solution.py
@@ -1,7 +1,7 @@
 import jax
 import jax.numpy as jnp
 from jax import lax
-from jax.sharding import PartitionSpec as P
+from jax.sharding import Mesh, PartitionSpec as P
 
 HIGH = lax.Precision.HIGHEST
 
@@ -71,19 +71,37 @@
     return jnp.concatenate([state, rate], axis=1)
 
 
+def swap_cores(array):
+    return lax.ppermute(array, "core", [(0, 1), (1, 0)])
+
+
 def carried_in(rates, state, initial_state):
-    length, mine = (lax.axis_size("seq"), lax.axis_index("seq"))
+    chips, chip = (lax.axis_size("chip"), lax.axis_index("chip"))
+    core = lax.axis_index("core")
+    half = state.shape[0] // 2
     own = pack(rates, state)
-    shifted = lax.ppermute(own, "seq", [(i, i + 1) for i in range(length - 1)])
-    first = pack(jnp.ones_like(rates), initial_state)
-    current = jnp.where(mine == 0, first, shifted)
+    own_mine = lax.dynamic_slice_in_dim(own, core * half, half, axis=0)
+    own_other = lax.dynamic_slice_in_dim(own, (1 - core) * half, half, axis=0)
+    partner_mine = swap_cores(own_other)
+    first_core = jnp.where(core == 0, own_mine, partner_mine)
+    second_core = jnp.where(core == 0, partner_mine, own_mine)
+    chip_element = link_packed(first_core, second_core)
+    shifted = lax.ppermute(chip_element, "chip", [(i, i + 1) for i in range(chips - 1)])
+    start_state = lax.dynamic_slice_in_dim(initial_state, core * half, half, axis=0)
+    first = pack(jnp.ones((half,), rates.dtype), start_state)
+    current = jnp.where(chip == 0, first, shifted)
     step = 1
-    while step < length:
-        earlier = lax.ppermute(current, "seq", [(i, i + step) for i in range(length - step)])
-        current = jnp.where(mine >= step, link_packed(earlier, current), current)
+    while step < chips:
+        earlier = lax.ppermute(current, "chip", [(i, i + step) for i in range(chips - step)])
+        current = jnp.where(chip >= step, link_packed(earlier, current), current)
         step *= 2
-    width = current.shape[1] - 128
-    return current[:, :width].reshape(state.shape)
+    for_second = link_packed(current, first_core)
+    keep = jnp.where(core == 0, current, for_second)
+    other = swap_cores(jnp.where(core == 0, for_second, current))
+    whole = jnp.where(core == 0, jnp.concatenate([keep, other]), jnp.concatenate([other, keep]))
+    width = whole.shape[1] - 128
+    return whole[:, :width].reshape(state.shape)
+
 
 def per_device(
     queries, key_vectors, value_rows, gate_logits, log_decay, initial_state, norm_gain, out_weight
@@ -114,29 +132,47 @@
     )
     attended = local_out + inherited
     hidden = normalize(attended, norm_gain, gate_logits)
-    terms = jnp.dot(
-        hidden,
-        lax.all_gather(out_weight, "seq", axis=1, tiled=True),
-        preferred_element_type=jnp.float32,
-    )
-    mixed = lax.psum_scatter(terms, "tensor", scatter_dimension=1, tiled=True)
+    chips, cores, groups = (lax.axis_size("chip"), lax.axis_size("core"), lax.axis_size("tensor"))
+    core = lax.axis_index("core")
+    seq_len = chips * cores
+    col_blocks = seq_len // groups
+    quarter = chips // col_blocks
+    route = []
+    for q in range(chips):
+        for c in range(cores):
+            for t in range(groups):
+                source = (col_blocks * t + q // quarter) * groups + (groups // cores) * c + q % quarter
+                route.append((source, (q * cores + c) * groups + t))
+    placed = lax.ppermute(out_weight, ("chip", "core", "tensor"), route)
+    columns = lax.all_gather(placed, "chip", axis=0, tiled=False)
+    columns = columns.reshape(col_blocks, -1, columns.shape[-1])
+    width = columns.shape[1]
+    full_hidden = lax.all_gather(hidden, "tensor", axis=1, tiled=True)
+    mine = lax.dynamic_slice_in_dim(full_hidden, core * width, width, axis=1)
+    theirs = swap_cores(lax.dynamic_slice_in_dim(full_hidden, (1 - core) * width, width, axis=1))
+    own_part = jnp.einsum("tk,rkc->trc", mine, columns, preferred_element_type=jnp.float32)
+    their_part = jnp.einsum("tk,rkc->trc", theirs, columns, preferred_element_type=jnp.float32)
+    mixed = (own_part + swap_cores(their_part)).reshape(rows_here, -1)
     return mixed
 
 
 def solution(mesh):
+    seq_len, groups = mesh.devices.shape
+    split = Mesh(mesh.devices.reshape(seq_len // 2, 2, groups), ("chip", "core", "tensor"))
+    tokens = ("chip", "core")
     return jax.shard_map(
         per_device,
-        mesh=mesh,
+        mesh=split,
         in_specs=(
-            P("seq", "tensor"),
-            P("seq", "tensor"),
-            P("seq", "tensor"),
-            P("seq", "tensor"),
-            P("seq", "tensor"),
+            P(tokens, "tensor"),
+            P(tokens, "tensor"),
+            P(tokens, "tensor"),
+            P(tokens, "tensor"),
+            P(tokens, "tensor"),
             P("tensor", None, None),
             P("tensor"),
-            P("tensor", "seq"),
+            P("tensor", tokens),
         ),
-        out_specs=P("seq", "tensor"),
+        out_specs=P(tokens, "tensor"),
         check_vma=False,
     )

time: 194 us -> 227 us (1.17)
  waiting for transfers between devices: 138 us -> 161 us
  starting transfers between devices: 22.3 us -> 30.9 us
  matrix products: 13.6 us -> 6.74 us
  local copies, waits for them, and re-layouts: 4.69 us -> 9.79 us
    all_gather x1 -> x2, waiting for transfers between devices: 4.19 us -> 85.4 us  [the longest x1 76.3 us: per_device(): columns = lax.all_gather(placed, 'chip', axis=0, tiled=False)]
    reduce_scatter x1 -> x0, waiting for transfers between devices: 52.9 us -> none  [per_device(): mixed = lax.psum_scatter(terms, 'tensor', scatter_dimension=1, tiled=True)]
    dot_general x1 -> x0, matrix products: 10.4 us -> none  [per_device(): jnp.dot(hidden, lax.all_gather(out_weight, 'seq', axis=1, tiled=True), pr...]
    ppermute x6 -> x10, starting transfers between devices: 22.3 us -> 30.9 us  [the longest x4 20 us: carried_in(): lax.ppermute(current, 'chip', [(i, i + step) for i in range(chips - step)])]
    ppermute x6 -> x10, waiting for transfers between devices: 81.1 us -> 75.6 us  [the longest x1 48.8 us: per_device(): placed = lax.ppermute(out_weight, ('chip', 'core', 'tensor'), route)]
    reshape x0 -> x2, local copies, waits for them, and re-layouts: none -> 4.12 us  [the longest x1 3.21 us: per_device(): columns = columns.reshape(col_blocks, -1, columns.shape[-1])]
    unnamed x0 -> x2, matrix products: none -> 3.59 us
  transfers between devices with their start and end apart: 8 -> 12, of which waited for: 8 -> 10; matrix products, arithmetic and copies ran while one was open for 3% -> 3% of each run, Pallas kernels for 0% -> 0%
where the time goes in v3:
time: 227 us; the launch traced here: 225 us
  waiting for transfers between devices  161 us (71%)
  starting transfers between devices  30.9 us (14%)
  between operations  13.8 us (6%)
  local copies, waits for them, and re-layouts  9.79 us (4%)
  matrix products  6.74 us (3%)
  other arithmetic  2.96 us (1%)
    all_gather x1, waiting for transfers between devices, per_device(): columns = lax.all_gather(placed, 'chip', axis=0, tiled=False)  76.3 us
    ppermute x1, waiting for transfers between devices, per_device(): placed = lax.ppermute(out_weight, ('chip', 'core', 'tensor'), route)  48.8 us
    ppermute x4, starting transfers between devices, carried_in(): lax.ppermute(current, 'chip', [(i, i + step) for i in range(chips - step)])  20 us
    ppermute x4, waiting for transfers between devices, carried_in(): lax.ppermute(current, 'chip', [(i, i + step) for i in range(chips - step)])  17.7 us
    all_gather x1, waiting for transfers between devices, per_device(): full_hidden = lax.all_gather(hidden, 'tensor', axis=1, tiled=True)  9.03 us
    ppermute x1, starting transfers between devices, per_device(): placed = lax.ppermute(out_weight, ('chip', 'core', 'tensor'), route)  7.4 us
    ppermute x1, waiting for transfers between devices, carried_in(): lax.ppermute(chip_element, 'chip', [(i, i + 1) for i in range(chips - 1)])  6.93 us
  transfers between devices with their start and end apart: 12, of which 10 were waited for; matrix products, arithmetic and copies ran while one was open for 3% of the time, Pallas kernels for 0%

profile of v3, /device:TPU:4, one launch (start us, length us, event | category | flops | bytes accessed | tf_op | source)
XLA Modules:
  0.0 225.3 jit_solution(5798322309535574056)
XLA Ops:
  6.5 0.8 copy.39
  7.6 1.1 copy.59
  8.8 1.4 fusion.4
  10.7 1.5 collective-permute-done
  12.7 3.1 %collective-permute-start.1 = (f32[4,16512]{1,0:T(4,128)S(1)}, f32[4,16512]{1,0:T(4,128)S(1)}, u32[]{:S(2)}, u32[]{:S(2)}) collective-permute-start(f32[4,16512]{1,0:T(4,128)S(1)} %pad_maximum_fusion.2), channel_id=1, source_target_pairs={{0,16},{16,32},{32,48},{48,64},{64,80},{80,96},{96,112},{112,128},... | collective-permute-start | bytes 792584 | tf_op jit(solution)/shard_map/ppermute | solution.py:89
  16.0 6.9 %collective-permute-done.1 = f32[4,16512]{1,0:T(4,128)S(1)} collective-permute-done((f32[4,16512]{1,0:T(4,128)S(1)}, f32[4,16512]{1,0:T(4,128)S(1)}, u32[]{:S(2)}, u32[]{:S(2)}) %collective-permute-start.1) | collective-permute-done | bytes 264224 | tf_op jit(solution)/shard_map/ppermute | solution.py:89
  23.0 3.1 %collective-permute-start.2 = (f32[4,16512]{1,0:T(4,128)S(1)}, f32[4,16512]{1,0:T(4,128)S(1)}, u32[]{:S(2)}, u32[]{:S(2)}) collective-permute-start(f32[4,16512]{1,0:T(4,128)S(1)} %pad_select_fusion), channel_id=1, source_target_pairs={{0,16},{16,32},{32,48},{48,64},{64,80},{80,96},{96,112},{112,128},... | collective-permute-start | bytes 792584 | tf_op jit(solution)/shard_map/ppermute | solution.py:95
  26.3 6.2 %collective-permute-done.2 = f32[4,16512]{1,0:T(4,128)S(1)} collective-permute-done((f32[4,16512]{1,0:T(4,128)S(1)}, f32[4,16512]{1,0:T(4,128)S(1)}, u32[]{:S(2)}, u32[]{:S(2)}) %collective-permute-start.2) | collective-permute-done | bytes 264224 | tf_op jit(solution)/shard_map/ppermute | solution.py:95
  32.7 7.6 %collective-permute-start.3 = (f32[4,16512]{1,0:T(4,128)S(1)}, f32[4,16512]{1,0:T(4,128)S(1)}, u32[]{:S(2)}, u32[]{:S(2)}) collective-permute-start(f32[4,16512]{1,0:T(4,128)S(1)} %maximum_select_fusion), channel_id=1, source_target_pairs={{0,32},{16,48},{32,64},{48,80},{64,96},{80,112},{96,128},{112,144}... | collective-permute-start | bytes 792584 | tf_op jit(solution)/shard_map/ppermute | solution.py:95
  40.5 4.1 %collective-permute-done.3 = f32[4,16512]{1,0:T(4,128)S(1)} collective-permute-done((f32[4,16512]{1,0:T(4,128)S(1)}, f32[4,16512]{1,0:T(4,128)S(1)}, u32[]{:S(2)}, u32[]{:S(2)}) %collective-permute-start.3) | collective-permute-done | bytes 264224 | tf_op jit(solution)/shard_map/ppermute | solution.py:95
  44.8 3.5 %collective-permute-start.4 = (f32[4,16512]{1,0:T(4,128)S(1)}, f32[4,16512]{1,0:T(4,128)S(1)}, u32[]{:S(2)}, u32[]{:S(2)}) collective-permute-start(f32[4,16512]{1,0:T(4,128)S(1)} %maximum_select_fusion.1), channel_id=1, source_target_pairs={{0,64},{16,80},{32,96},{48,112},{64,128},{80,144},{96,160},{112,17... | collective-permute-start | bytes 792584 | tf_op jit(solution)/shard_map/ppermute | solution.py:95
  48.4 3.8 %collective-permute-done.4 = f32[4,16512]{1,0:T(4,128)S(1)} collective-permute-done((f32[4,16512]{1,0:T(4,128)S(1)}, f32[4,16512]{1,0:T(4,128)S(1)}, u32[]{:S(2)}, u32[]{:S(2)}) %collective-permute-start.4) | collective-permute-done | bytes 264224 | tf_op jit(solution)/shard_map/ppermute | solution.py:95
  52.4 5.8 %collective-permute-start.5 = (f32[4,16512]{1,0:T(4,128)S(1)}, f32[4,16512]{1,0:T(4,128)S(1)}, u32[]{:S(2)}, u32[]{:S(2)}) collective-permute-start(f32[4,16512]{1,0:T(4,128)S(1)} %maximum_select_fusion.2), channel_id=1, source_target_pairs={{0,128},{16,144},{32,160},{48,176},{64,192},{80,208},{96,224},{112... | collective-permute-start | bytes 792584 | tf_op jit(solution)/shard_map/ppermute | solution.py:95
  58.4 3.6 %collective-permute-done.5 = f32[4,16512]{1,0:T(4,128)S(1)} collective-permute-done((f32[4,16512]{1,0:T(4,128)S(1)}, f32[4,16512]{1,0:T(4,128)S(1)}, u32[]{:S(2)}, u32[]{:S(2)}) %collective-permute-start.5) | collective-permute-done | bytes 264224 | tf_op jit(solution)/shard_map/ppermute | solution.py:95
  65.8 0.9 multiply_convert_fusion
  66.7 7.4 %collective-permute-start.7 = (bf16[1024,192]{0,1:T(8,128)(2,1)}, bf16[1024,192]{0,1:T(8,128)(2,1)S(1)}, u32[]{:S(2)}, u32[]{:S(2)}) collective-permute-start(bf16[1024,192]{0,1:T(8,128)(2,1)} %param.15), channel_id=1, source_target_pairs={{0,0},{32,1},{64,2},{96,3},{128,4},{160,5},{192,6},{224,7},{4,8},{... | collective-permute-start | bytes 1179656 | tf_op jit(solution)/shard_map/ppermute | solution.py:146
  74.1 48.8 %collective-permute-done.7 = bf16[1024,192]{0,1:T(8,128)(2,1)S(1)} collective-permute-done((bf16[1024,192]{0,1:T(8,128)(2,1)}, bf16[1024,192]{0,1:T(8,128)(2,1)S(1)}, u32[]{:S(2)}, u32[]{:S(2)}) %collective-permute-start.7) | collective-permute-done | bytes 393248 | tf_op jit(solution)/shard_map/ppermute | solution.py:146
  123.8 9.0 %all-gather.4.cloned.1.call-done = bf16[128,8192]{1,0:T(8,128)(2,1)} async-done(((bf16[128,1024]{1,0:T(8,128)(2,1)}), bf16[128,8192]{1,0:T(8,128)(2,1)}) %all-gather.4.cloned.1.call-update) | async-done | bytes 2097168 | tf_op jit(solution)/shard_map/all_gather | solution.py:150
  132.8 1.3 constant_dynamic-slice_fusion
  134.2 76.3 %all-gather.6.cloned.1.call-done = bf16[16384,192]{0,1:T(8,128)(2,1)} async-done(((bf16[1024,192]{0,1:T(8,128)(2,1)}), bf16[16384,192]{0,1:T(8,128)(2,1)}) %all-gather.6.cloned.1.call-update) | async-done | bytes 6291472 | tf_op jit(solution)/shard_map/all_gather | solution.py:147
  210.5 3.2 %copy.98 = bf16[24,4,8,4096]{3,2,0,1:T(8,128)(2,1)S(1)} copy(bf16[24,4,8,4096]{3,2,1,0:T(8,128)(2,1)} %bitcast.91) | data formatting | bytes 12582912 | tf_op jit(solution)/shard_map/reshape | solution.py:148
  213.8 1.8 fusion.48
  215.7 1.8 fusion.6
  217.5 0.9 copy.56
  (72 shorter events, 7.4 us)
Async XLA Ops:
  6.5 9.2 %copy-start = (f32[8,128,128]{2,1,0:T(8,128)S(1)}, f32[8,128,128]{2,1,0:T(8,128)}, u32[]{:S(2)}) copy-start(f32[8,128,128]{2,1,0:T(8,128)} %param.13) | copy-start | bytes 1572868
  6.5 126.2 %all-gather.4.cloned.1.call-start = ((), (), s32[]{:S(2)}) async-start(), calls=%async_computation | async-start | bytes 2359296 | tf_op jit(solution)/shard_map/all_gather | solution.py:150
  10.6 1.6 collective-permute-start
  10.7 52.1 %copy-start.1 = (bf16[128,1024]{1,0:T(8,128)(2,1)S(1)}, bf16[128,1024]{1,0:T(8,128)(2,1)}, u32[]{:S(2)}) copy-start(bf16[128,1024]{1,0:T(8,128)(2,1)} %param.8) | copy-start | bytes 786436
  12.7 10.3 %collective-permute-start.1 = (f32[4,16512]{1,0:T(4,128)S(1)}, f32[4,16512]{1,0:T(4,128)S(1)}, u32[]{:S(2)}, u32[]{:S(2)}) collective-permute-start(f32[4,16512]{1,0:T(4,128)S(1)} %pad_maximum_fusion.2), channel_id=1, source_target_pairs={{0,16},{16,32},{32,48},{48,64},{64,80},{80,96},{96,112},{112,128},... | collective-permute-start | bytes 792584 | tf_op jit(solution)/shard_map/ppermute | solution.py:89
  16.0 49.0 %copy-start.3 = (bf16[128,1024]{1,0:T(8,128)(2,1)S(1)}, bf16[128,1024]{1,0:T(8,128)(2,1)}, u32[]{:S(2)}) copy-start(bf16[128,1024]{1,0:T(8,128)(2,1)} %param.10) | copy-start | bytes 786436
  23.0 9.4 %collective-permute-start.2 = (f32[4,16512]{1,0:T(4,128)S(1)}, f32[4,16512]{1,0:T(4,128)S(1)}, u32[]{:S(2)}, u32[]{:S(2)}) collective-permute-start(f32[4,16512]{1,0:T(4,128)S(1)} %pad_select_fusion), channel_id=1, source_target_pairs={{0,16},{16,32},{32,48},{48,64},{64,80},{80,96},{96,112},{112,128},... | collective-permute-start | bytes 792584 | tf_op jit(solution)/shard_map/ppermute | solution.py:95
  32.7 11.8 %collective-permute-start.3 = (f32[4,16512]{1,0:T(4,128)S(1)}, f32[4,16512]{1,0:T(4,128)S(1)}, u32[]{:S(2)}, u32[]{:S(2)}) collective-permute-start(f32[4,16512]{1,0:T(4,128)S(1)} %maximum_select_fusion), channel_id=1, source_target_pairs={{0,32},{16,48},{32,64},{48,80},{64,96},{80,112},{96,128},{112,144}... | collective-permute-start | bytes 792584 | tf_op jit(solution)/shard_map/ppermute | solution.py:95
  44.8 7.4 %collective-permute-start.4 = (f32[4,16512]{1,0:T(4,128)S(1)}, f32[4,16512]{1,0:T(4,128)S(1)}, u32[]{:S(2)}, u32[]{:S(2)}) collective-permute-start(f32[4,16512]{1,0:T(4,128)S(1)} %maximum_select_fusion.1), channel_id=1, source_target_pairs={{0,64},{16,80},{32,96},{48,112},{64,128},{80,144},{96,160},{112,17... | collective-permute-start | bytes 792584 | tf_op jit(solution)/shard_map/ppermute | solution.py:95
  52.2 13.6 %copy-start.5 = (bf16[128,1024]{1,0:T(8,128)(2,1)S(1)}, bf16[128,1024]{1,0:T(8,128)(2,1)}, u32[]{:S(2)}) copy-start(bf16[128,1024]{1,0:T(8,128)(2,1)} %param.11) | copy-start | bytes 786436
  52.2 13.6 %copy-start.6 = (f32[1024]{0:T(1024)S(1)}, f32[1024]{0:T(1024)}, u32[]{:S(2)}) copy-start(f32[1024]{0:T(1024)} %param.14) | copy-start | bytes 12292
  52.4 9.6 %collective-permute-start.5 = (f32[4,16512]{1,0:T(4,128)S(1)}, f32[4,16512]{1,0:T(4,128)S(1)}, u32[]{:S(2)}, u32[]{:S(2)}) collective-permute-start(f32[4,16512]{1,0:T(4,128)S(1)} %maximum_select_fusion.2), channel_id=1, source_target_pairs={{0,128},{16,144},{32,160},{48,176},{64,192},{80,208},{96,224},{112... | collective-permute-start | bytes 792584 | tf_op jit(solution)/shard_map/ppermute | solution.py:95
  62.5 1.6 collective-permute-start.6
  66.7 143.8 %all-gather.6.cloned.1.call-start = ((), (), s32[]{:S(2)}) async-start(), calls=%async_computation.1 | async-start | bytes 6684672 | tf_op jit(solution)/shard_map/all_gather | solution.py:147
  66.7 56.3 %collective-permute-start.7 = (bf16[1024,192]{0,1:T(8,128)(2,1)}, bf16[1024,192]{0,1:T(8,128)(2,1)S(1)}, u32[]{:S(2)}, u32[]{:S(2)}) collective-permute-start(bf16[1024,192]{0,1:T(8,128)(2,1)} %param.15), channel_id=1, source_target_pairs={{0,0},{32,1},{64,2},{96,3},{128,4},{160,5},{192,6},{224,7},{4,8},{... | collective-permute-start | bytes 1179656 | tf_op jit(solution)/shard_map/ppermute | solution.py:146
  123.0 0.7 copy-start.4
  134.1 79.7 %collective-permute-start.8 = (bf16[128,4096]{1,0:T(8,128)(2,1)S(1)}, bf16[128,4096]{1,0:T(8,128)(2,1)S(1)}, u32[]{:S(2)}, u32[]{:S(2)}) collective-permute-start(bf16[128,4096]{1,0:T(8,128)(2,1)S(1)} %constant_dynamic-slice_fusion), channel_id=1, source_target_pairs={{0,8},{8,0},{1,9},{9,1},{2,10},{10,2},{3,11},{11,3},{4,12},{12,4},... | collective-permute-start | bytes 3145736 | tf_op jit(solution)/shard_map/ppermute | solution.py:75
  213.7 1.9 copy-start.2
  215.5 1.9 collective-permute-start.9
Sparse Core Ops, SparseCore 0:
  66.8 65.9 all-gather.3
  135.2 75.2 all-gather.5

commit v4 on v3

--- a/solution.py
+++ b/solution.py
@@ -103,6 +103,35 @@
     return whole[:, :width].reshape(state.shape)
 
 
+def place_columns(out_weight):
+    chips, cores, groups = (lax.axis_size("chip"), lax.axis_size("core"), lax.axis_size("tensor"))
+    col_blocks = chips * cores // groups
+    quarter = chips // col_blocks
+    route = []
+    for q in range(chips):
+        for c in range(cores):
+            for t in range(groups):
+                source = (col_blocks * t + q // quarter) * groups + (groups // cores) * c + q % quarter
+                route.append((source, (q * cores + c) * groups + t))
+    return lax.ppermute(out_weight, ("chip", "core", "tensor"), route)
+
+
+def gather_groups(block):
+    groups, mine = (lax.axis_size("tensor"), lax.axis_index("tensor"))
+    up = [(i, (i + 1) % groups) for i in range(groups)]
+    down = [(i, (i - 1) % groups) for i in range(groups)]
+    from_below, from_above = [], []
+    below, above = block, block
+    for _ in range(groups // 2):
+        below = lax.ppermute(below, "tensor", up)
+        from_below.append(below)
+        if len(from_above) < (groups - 1) // 2:
+            above = lax.ppermute(above, "tensor", down)
+            from_above.append(above)
+    relative = jnp.concatenate([block] + from_above + from_below[::-1], axis=1)
+    return jnp.roll(relative, mine * block.shape[1], axis=1)
+
+
 def per_device(
     queries, key_vectors, value_rows, gate_logits, log_decay, initial_state, norm_gain, out_weight
 ):
@@ -115,6 +144,8 @@
     def shaped(array):
         return array.reshape(block_count, block_len, head_count, head_dim)
 
+    placed = place_columns(out_weight)
+    placed, queries = lax.optimization_barrier((placed, queries))
     zero_state = jnp.zeros((head_count, head_dim, head_dim), jnp.float32)
     decay_blocks = log_decay.reshape(block_count, block_len, head_count)
     device_state, outputs = lax.scan(
@@ -137,17 +168,10 @@
     seq_len = chips * cores
     col_blocks = seq_len // groups
     quarter = chips // col_blocks
-    route = []
-    for q in range(chips):
-        for c in range(cores):
-            for t in range(groups):
-                source = (col_blocks * t + q // quarter) * groups + (groups // cores) * c + q % quarter
-                route.append((source, (q * cores + c) * groups + t))
-    placed = lax.ppermute(out_weight, ("chip", "core", "tensor"), route)
     columns = lax.all_gather(placed, "chip", axis=0, tiled=False)
     columns = columns.reshape(col_blocks, -1, columns.shape[-1])
     width = columns.shape[1]
-    full_hidden = lax.all_gather(hidden, "tensor", axis=1, tiled=True)
+    full_hidden = gather_groups(hidden)
     mine = lax.dynamic_slice_in_dim(full_hidden, core * width, width, axis=1)
     theirs = swap_cores(lax.dynamic_slice_in_dim(full_hidden, (1 - core) * width, width, axis=1))
     own_part = jnp.einsum("tk,rkc->trc", mine, columns, preferred_element_type=jnp.float32)

time: 227 us -> 193 us (0.85)
  waiting for transfers between devices: 161 us -> 98.2 us
  starting transfers between devices: 30.9 us -> 46.3 us
  local copies, waits for them, and re-layouts: 9.79 us -> 21.4 us
    all_gather x1, waiting for transfers between devices: 76.3 us -> 18.3 us  [per_device(): columns = lax.all_gather(placed, 'chip', axis=0, tiled=False)]
    ppermute x1 -> x8, waiting for transfers between devices: 48.8 us -> 60.4 us  [the longest x1 37.8 us: place_columns(): return lax.ppermute(out_weight, ('chip', 'core', 'tensor'), route)]
    ppermute x1 -> x8, starting transfers between devices: 7.4 us -> 18.9 us  [the longest x3 9.7 us: gather_groups(): above = lax.ppermute(above, 'tensor', down)]
    unnamed x18 -> x30, local copies, waits for them, and re-layouts: 2.13 us -> 12.6 us
    all_gather x1 -> x0, waiting for transfers between devices: 9.03 us -> none  [per_device(): full_hidden = lax.all_gather(hidden, 'tensor', axis=1, tiled=True)]
    ppermute x4, waiting for transfers between devices: 17.7 us -> 10.3 us  [carried_in(): lax.ppermute(current, 'chip', [(i, i + step) for i in range(chips - step)])]
    ppermute x4, starting transfers between devices: 20 us -> 24 us  [carried_in(): lax.ppermute(current, 'chip', [(i, i + step) for i in range(chips - step)])]
  transfers between devices with their start and end apart: 12 -> 18, of which waited for: 10 -> 12; matrix products, arithmetic and copies ran while one was open for 3% -> 13% of each run, Pallas kernels for 0% -> 0%
where the time goes in v4:
time: 193 us; the launch traced here: 191 us
  waiting for transfers between devices  98.2 us (51%)
  starting transfers between devices  46.3 us (24%)
  local copies, waits for them, and re-layouts  21.4 us (11%)
  between operations  13.8 us (7%)
  matrix products  8.06 us (4%)
  other arithmetic  2.98 us (2%)
    ppermute x1, waiting for transfers between devices, place_columns(): return lax.ppermute(out_weight, ('chip', 'core', 'tensor'), route)  37.8 us
    ppermute x4, starting transfers between devices, carried_in(): lax.ppermute(current, 'chip', [(i, i + step) for i in range(chips - step)])  24 us
    ppermute x4, waiting for transfers between devices, gather_groups(): below = lax.ppermute(below, 'tensor', up)  21.6 us
    all_gather x1, waiting for transfers between devices, per_device(): columns = lax.all_gather(placed, 'chip', axis=0, tiled=False)  18.3 us
    unnamed x30, local copies, waits for them, and re-layouts  12.6 us
    ppermute x4, waiting for transfers between devices, carried_in(): lax.ppermute(current, 'chip', [(i, i + step) for i in range(chips - step)])  10.3 us
    ppermute x3, starting transfers between devices, gather_groups(): above = lax.ppermute(above, 'tensor', down)  9.7 us
    ppermute x1, starting transfers between devices, place_columns(): return lax.ppermute(out_weight, ('chip', 'core', 'tensor'), route)  7.14 us
  transfers between devices with their start and end apart: 18, of which 12 were waited for; matrix products, arithmetic and copies ran while one was open for 13% of the time, Pallas kernels for 0%

profile of v4, /device:TPU:4, one launch (start us, length us, event | category | flops | bytes accessed | tf_op | source)
XLA Modules:
  0.0 190.7 jit_solution(2439229120185232188)
XLA Ops:
  10.7 1.5 collective-permute-done.1
  12.7 3.1 %collective-permute-start.2 = (f32[4,16512]{1,0:T(4,128)S(1)}, f32[4,16512]{1,0:T(4,128)S(1)}, u32[]{:S(2)}, u32[]{:S(2)}) collective-permute-start(f32[4,16512]{1,0:T(4,128)S(1)} %pad_maximum_fusion.2), channel_id=1, source_target_pairs={{0,16},{16,32},{32,48},{48,64},{64,80},{80,96},{96,112},{112,128},... | collective-permute-start | bytes 792584 | tf_op jit(solution)/shard_map/ppermute | solution.py:89
  16.0 6.9 %collective-permute-done.2 = f32[4,16512]{1,0:T(4,128)S(1)} collective-permute-done((f32[4,16512]{1,0:T(4,128)S(1)}, f32[4,16512]{1,0:T(4,128)S(1)}, u32[]{:S(2)}, u32[]{:S(2)}) %collective-permute-start.2) | collective-permute-done | bytes 264224 | tf_op jit(solution)/shard_map/ppermute | solution.py:89
  23.0 3.1 %collective-permute-start.3 = (f32[4,16512]{1,0:T(4,128)S(1)}, f32[4,16512]{1,0:T(4,128)S(1)}, u32[]{:S(2)}, u32[]{:S(2)}) collective-permute-start(f32[4,16512]{1,0:T(4,128)S(1)} %pad_select_fusion), channel_id=1, source_target_pairs={{0,16},{16,32},{32,48},{48,64},{64,80},{80,96},{96,112},{112,128},... | collective-permute-start | bytes 792584 | tf_op jit(solution)/shard_map/ppermute | solution.py:95
  26.3 6.2 %collective-permute-done.3 = f32[4,16512]{1,0:T(4,128)S(1)} collective-permute-done((f32[4,16512]{1,0:T(4,128)S(1)}, f32[4,16512]{1,0:T(4,128)S(1)}, u32[]{:S(2)}, u32[]{:S(2)}) %collective-permute-start.3) | collective-permute-done | bytes 264224 | tf_op jit(solution)/shard_map/ppermute | solution.py:95
  32.7 7.6 %collective-permute-start.4 = (f32[4,16512]{1,0:T(4,128)S(1)}, f32[4,16512]{1,0:T(4,128)S(1)}, u32[]{:S(2)}, u32[]{:S(2)}) collective-permute-start(f32[4,16512]{1,0:T(4,128)S(1)} %maximum_select_fusion), channel_id=1, source_target_pairs={{0,32},{16,48},{32,64},{48,80},{64,96},{80,112},{96,128},{112,144}... | collective-permute-start | bytes 792584 | tf_op jit(solution)/shard_map/ppermute | solution.py:95
  40.5 4.1 %collective-permute-done.4 = f32[4,16512]{1,0:T(4,128)S(1)} collective-permute-done((f32[4,16512]{1,0:T(4,128)S(1)}, f32[4,16512]{1,0:T(4,128)S(1)}, u32[]{:S(2)}, u32[]{:S(2)}) %collective-permute-start.4) | collective-permute-done | bytes 264224 | tf_op jit(solution)/shard_map/ppermute | solution.py:95
  44.8 3.5 %collective-permute-start.5 = (f32[4,16512]{1,0:T(4,128)S(1)}, f32[4,16512]{1,0:T(4,128)S(1)}, u32[]{:S(2)}, u32[]{:S(2)}) collective-permute-start(f32[4,16512]{1,0:T(4,128)S(1)} %maximum_select_fusion.1), channel_id=1, source_target_pairs={{0,64},{16,80},{32,96},{48,112},{64,128},{80,144},{96,160},{112,17... | collective-permute-start | bytes 792584 | tf_op jit(solution)/shard_map/ppermute | solution.py:95
  48.3 7.1 %collective-permute-start = (bf16[1024,192]{0,1:T(8,128)(2,1)}, bf16[1024,192]{0,1:T(8,128)(2,1)S(1)}, u32[]{:S(2)}, u32[]{:S(2)}) collective-permute-start(bf16[1024,192]{0,1:T(8,128)(2,1)} %param.15), channel_id=1, source_target_pairs={{0,0},{32,1},{64,2},{96,3},{128,4},{160,5},{192,6},{224,7},{4,8},{... | collective-permute-start | bytes 1179656 | tf_op jit(solution)/shard_map/ppermute | solution.py:116
  55.8 9.7 %collective-permute-start.6 = (f32[4,16512]{1,0:T(4,128)S(1)}, f32[4,16512]{1,0:T(4,128)S(1)}, u32[]{:S(2)}, u32[]{:S(2)}) collective-permute-start(f32[4,16512]{1,0:T(4,128)S(1)} %maximum_select_fusion.2), channel_id=1, source_target_pairs={{0,128},{16,144},{32,160},{48,176},{64,192},{80,208},{96,224},{112... | collective-permute-start | bytes 792584 | tf_op jit(solution)/shard_map/ppermute | solution.py:95
  65.7 37.8 %collective-permute-done = bf16[1024,192]{0,1:T(8,128)(2,1)S(1)} collective-permute-done((bf16[1024,192]{0,1:T(8,128)(2,1)}, bf16[1024,192]{0,1:T(8,128)(2,1)S(1)}, u32[]{:S(2)}, u32[]{:S(2)}) %collective-permute-start) | collective-permute-done | bytes 393248 | tf_op jit(solution)/shard_map/ppermute | solution.py:116
  109.0 3.2 %collective-permute-start.8 = (bf16[128,1024]{1,0:T(8,128)(2,1)S(1)}, bf16[128,1024]{1,0:T(8,128)(2,1)S(1)}, u32[]{:S(2)}, u32[]{:S(2)}) collective-permute-start(bf16[128,1024]{1,0:T(8,128)(2,1)S(1)} %get-tuple-element.30), channel_id=1, source_target_pairs={{0,7},{1,0},{2,1},{3,2},{4,3},{5,4},{6,5},{7,6},{8,15},{9,8},{10,9... | collective-permute-start | bytes 786440 | tf_op jit(solution)/shard_map/ppermute | solution.py:129
  112.3 6.3 %collective-permute-done.11 = bf16[128,1024]{1,0:T(8,128)(2,1)S(1)} collective-permute-done((bf16[128,1024]{1,0:T(8,128)(2,1)S(1)}, bf16[128,1024]{1,0:T(8,128)(2,1)S(1)}, u32[]{:S(2)}, u32[]{:S(2)}) %collective-permute-start.11) | collective-permute-done | bytes 262176 | tf_op jit(solution)/shard_map/ppermute | solution.py:126
  118.6 3.2 %collective-permute-start.9 = (bf16[128,1024]{1,0:T(8,128)(2,1)S(1)}, bf16[128,1024]{1,0:T(8,128)(2,1)S(1)}, u32[]{:S(2)}, u32[]{:S(2)}) collective-permute-start(bf16[128,1024]{1,0:T(8,128)(2,1)S(1)} %collective-permute-done.8), channel_id=1, source_target_pairs={{0,7},{1,0},{2,1},{3,2},{4,3},{5,4},{6,5},{7,6},{8,15},{9,8},{10,9... | collective-permute-start | bytes 786440 | tf_op jit(solution)/shard_map/ppermute | solution.py:129
  121.8 5.5 %collective-permute-done.12 = bf16[128,1024]{1,0:T(8,128)(2,1)S(1)} collective-permute-done((bf16[128,1024]{1,0:T(8,128)(2,1)S(1)}, bf16[128,1024]{1,0:T(8,128)(2,1)S(1)}, u32[]{:S(2)}, u32[]{:S(2)}) %collective-permute-start.12) | collective-permute-done | bytes 262176 | tf_op jit(solution)/shard_map/ppermute | solution.py:126
  127.3 3.2 %collective-permute-start.10 = (bf16[128,1024]{1,0:T(8,128)(2,1)S(1)}, bf16[128,1024]{1,0:T(8,128)(2,1)S(1)}, u32[]{:S(2)}, u32[]{:S(2)}) collective-permute-start(bf16[128,1024]{1,0:T(8,128)(2,1)S(1)} %collective-permute-done.9), channel_id=1, source_target_pairs={{0,7},{1,0},{2,1},{3,2},{4,3},{5,4},{6,5},{7,6},{8,15},{9,8},{10,9... | collective-permute-start | bytes 786440 | tf_op jit(solution)/shard_map/ppermute | solution.py:129
  130.5 4.7 %collective-permute-done.13 = bf16[128,1024]{1,0:T(8,128)(2,1)S(1)} collective-permute-done((bf16[128,1024]{1,0:T(8,128)(2,1)S(1)}, bf16[128,1024]{1,0:T(8,128)(2,1)S(1)}, u32[]{:S(2)}, u32[]{:S(2)}) %collective-permute-start.13) | collective-permute-done | bytes 262176 | tf_op jit(solution)/shard_map/ppermute | solution.py:126
  135.2 2.0 %collective-permute-start.14 = (bf16[128,1024]{1,0:T(8,128)(2,1)S(1)}, bf16[128,1024]{1,0:T(8,128)(2,1)S(1)}, u32[]{:S(2)}, u32[]{:S(2)}) collective-permute-start(bf16[128,1024]{1,0:T(8,128)(2,1)S(1)} %collective-permute-done.13), channel_id=1, source_target_pairs={{0,1},{1,2},{2,3},{3,4},{4,5},{5,6},{6,7},{7,0},{8,9},{9,10},{10,1... | collective-permute-start | bytes 786440 | tf_op jit(solution)/shard_map/ppermute | solution.py:126
  140.6 5.1 %collective-permute-done.14 = bf16[128,1024]{1,0:T(8,128)(2,1)S(1)} collective-permute-done((bf16[128,1024]{1,0:T(8,128)(2,1)S(1)}, bf16[128,1024]{1,0:T(8,128)(2,1)S(1)}, u32[]{:S(2)}, u32[]{:S(2)}) %collective-permute-start.14) | collective-permute-done | bytes 262176 | tf_op jit(solution)/shard_map/ppermute | solution.py:126
  154.6 1.6 constant_dynamic-slice_fusion
  156.3 18.3 %all-gather.3.cloned.1.call-done = bf16[16384,192]{0,1:T(8,128)(2,1)} async-done(((bf16[1024,192]{0,1:T(8,128)(2,1)}), bf16[16384,192]{0,1:T(8,128)(2,1)}) %all-gather.3.cloned.1.call-update) | async-done | bytes 6291472 | tf_op jit(solution)/shard_map/all_gather | solution.py:171
  174.6 3.2 %copy.98 = bf16[24,4,8,4096]{3,2,0,1:T(8,128)(2,1)S(1)} copy(bf16[24,4,8,4096]{3,2,1,0:T(8,128)(2,1)} %bitcast.91) | data formatting | bytes 12582912 | tf_op jit(solution)/shard_map/reshape | solution.py:172
  177.9 1.8 fusion.48
  179.8 3.1 %fusion.6 = f32[128,768]{0,1:S(1)} fusion(bf16[4096,768]{0,1:T(8,128)(2,1)S(1)} %bitcast.90, bf16[128,16384]{1,0:T(8,128)(2,1)} %constant_dynamic-update-slice_fusion, s32[]{:T(128)S(6)} %dynamic_slice.36), kind=kOutput, calls=%fused_computation.12 | convolution fusion | flops 805306368 | bytes 7733252
  (96 shorter events, 24.8 us)
Async XLA Ops:
  6.5 9.2 %copy-start = (f32[8,128,128]{2,1,0:T(8,128)S(1)}, f32[8,128,128]{2,1,0:T(8,128)}, u32[]{:S(2)}) copy-start(f32[8,128,128]{2,1,0:T(8,128)} %param.13) | copy-start | bytes 1572868
  6.5 168.1 %all-gather.3.cloned.1.call-start = ((), (), s32[]{:S(2)}) async-start(), calls=%async_computation | async-start | bytes 6684672 | tf_op jit(solution)/shard_map/all_gather | solution.py:171
  10.6 1.6 collective-permute-start.1
  12.7 10.3 %collective-permute-start.2 = (f32[4,16512]{1,0:T(4,128)S(1)}, f32[4,16512]{1,0:T(4,128)S(1)}, u32[]{:S(2)}, u32[]{:S(2)}) collective-permute-start(f32[4,16512]{1,0:T(4,128)S(1)} %pad_maximum_fusion.2), channel_id=1, source_target_pairs={{0,16},{16,32},{32,48},{48,64},{64,80},{80,96},{96,112},{112,128},... | collective-permute-start | bytes 792584 | tf_op jit(solution)/shard_map/ppermute | solution.py:89
  23.0 9.4 %collective-permute-start.3 = (f32[4,16512]{1,0:T(4,128)S(1)}, f32[4,16512]{1,0:T(4,128)S(1)}, u32[]{:S(2)}, u32[]{:S(2)}) collective-permute-start(f32[4,16512]{1,0:T(4,128)S(1)} %pad_select_fusion), channel_id=1, source_target_pairs={{0,16},{16,32},{32,48},{48,64},{64,80},{80,96},{96,112},{112,128},... | collective-permute-start | bytes 792584 | tf_op jit(solution)/shard_map/ppermute | solution.py:95
  32.5 72.7 %copy-start.1 = (bf16[128,1024]{1,0:T(8,128)(2,1)S(1)}, bf16[128,1024]{1,0:T(8,128)(2,1)}, u32[]{:S(2)}) copy-start(bf16[128,1024]{1,0:T(8,128)(2,1)} %param.8) | copy-start | bytes 786436
  32.7 11.8 %collective-permute-start.4 = (f32[4,16512]{1,0:T(4,128)S(1)}, f32[4,16512]{1,0:T(4,128)S(1)}, u32[]{:S(2)}, u32[]{:S(2)}) collective-permute-start(f32[4,16512]{1,0:T(4,128)S(1)} %maximum_select_fusion), channel_id=1, source_target_pairs={{0,32},{16,48},{32,64},{48,80},{64,96},{80,112},{96,128},{112,144}... | collective-permute-start | bytes 792584 | tf_op jit(solution)/shard_map/ppermute | solution.py:95
  44.8 10.8 %collective-permute-start.5 = (f32[4,16512]{1,0:T(4,128)S(1)}, f32[4,16512]{1,0:T(4,128)S(1)}, u32[]{:S(2)}, u32[]{:S(2)}) collective-permute-start(f32[4,16512]{1,0:T(4,128)S(1)} %maximum_select_fusion.1), channel_id=1, source_target_pairs={{0,64},{16,80},{32,96},{48,112},{64,128},{80,144},{96,160},{112,17... | collective-permute-start | bytes 792584 | tf_op jit(solution)/shard_map/ppermute | solution.py:95
  48.3 55.2 %collective-permute-start = (bf16[1024,192]{0,1:T(8,128)(2,1)}, bf16[1024,192]{0,1:T(8,128)(2,1)S(1)}, u32[]{:S(2)}, u32[]{:S(2)}) collective-permute-start(bf16[1024,192]{0,1:T(8,128)(2,1)} %param.15), channel_id=1, source_target_pairs={{0,0},{32,1},{64,2},{96,3},{128,4},{160,5},{192,6},{224,7},{4,8},{... | collective-permute-start | bytes 1179656 | tf_op jit(solution)/shard_map/ppermute | solution.py:116
  55.6 51.8 %copy-start.2 = (bf16[128,1024]{1,0:T(8,128)(2,1)S(1)}, bf16[128,1024]{1,0:T(8,128)(2,1)}, u32[]{:S(2)}) copy-start(bf16[128,1024]{1,0:T(8,128)(2,1)} %param.10) | copy-start | bytes 786436
  55.8 48.6 %collective-permute-start.6 = (f32[4,16512]{1,0:T(4,128)S(1)}, f32[4,16512]{1,0:T(4,128)S(1)}, u32[]{:S(2)}, u32[]{:S(2)}) collective-permute-start(f32[4,16512]{1,0:T(4,128)S(1)} %maximum_select_fusion.2), channel_id=1, source_target_pairs={{0,128},{16,144},{32,160},{48,176},{64,192},{80,208},{96,224},{112... | collective-permute-start | bytes 792584 | tf_op jit(solution)/shard_map/ppermute | solution.py:95
  103.5 0.7 copy-start.3
  104.8 3.4 %copy-start.4 = (bf16[128,1024]{1,0:T(8,128)(2,1)S(1)}, bf16[128,1024]{1,0:T(8,128)(2,1)}, u32[]{:S(2)}) copy-start(bf16[128,1024]{1,0:T(8,128)(2,1)} %param.11) | copy-start | bytes 786436
  104.8 3.4 %copy-start.5 = (f32[1024]{0:T(1024)S(1)}, f32[1024]{0:T(1024)}, u32[]{:S(2)}) copy-start(f32[1024]{0:T(1024)} %param.14) | copy-start | bytes 12292
  104.9 1.6 collective-permute-start.7
  109.0 9.6 %collective-permute-start.11 = (bf16[128,1024]{1,0:T(8,128)(2,1)S(1)}, bf16[128,1024]{1,0:T(8,128)(2,1)S(1)}, u32[]{:S(2)}, u32[]{:S(2)}) collective-permute-start(bf16[128,1024]{1,0:T(8,128)(2,1)S(1)} %get-tuple-element.30), channel_id=1, source_target_pairs={{0,1},{1,2},{2,3},{3,4},{4,5},{5,6},{6,7},{7,0},{8,9},{9,10},{10,1... | collective-permute-start | bytes 786440 | tf_op jit(solution)/shard_map/ppermute | solution.py:126
  109.0 9.6 %collective-permute-start.8 = (bf16[128,1024]{1,0:T(8,128)(2,1)S(1)}, bf16[128,1024]{1,0:T(8,128)(2,1)S(1)}, u32[]{:S(2)}, u32[]{:S(2)}) collective-permute-start(bf16[128,1024]{1,0:T(8,128)(2,1)S(1)} %get-tuple-element.30), channel_id=1, source_target_pairs={{0,7},{1,0},{2,1},{3,2},{4,3},{5,4},{6,5},{7,6},{8,15},{9,8},{10,9... | collective-permute-start | bytes 786440 | tf_op jit(solution)/shard_map/ppermute | solution.py:129
  118.6 8.7 %collective-permute-start.12 = (bf16[128,1024]{1,0:T(8,128)(2,1)S(1)}, bf16[128,1024]{1,0:T(8,128)(2,1)S(1)}, u32[]{:S(2)}, u32[]{:S(2)}) collective-permute-start(bf16[128,1024]{1,0:T(8,128)(2,1)S(1)} %collective-permute-done.11), channel_id=1, source_target_pairs={{0,1},{1,2},{2,3},{3,4},{4,5},{5,6},{6,7},{7,0},{8,9},{9,10},{10,1... | collective-permute-start | bytes 786440 | tf_op jit(solution)/shard_map/ppermute | solution.py:126
  118.6 8.7 %collective-permute-start.9 = (bf16[128,1024]{1,0:T(8,128)(2,1)S(1)}, bf16[128,1024]{1,0:T(8,128)(2,1)S(1)}, u32[]{:S(2)}, u32[]{:S(2)}) collective-permute-start(bf16[128,1024]{1,0:T(8,128)(2,1)S(1)} %collective-permute-done.8), channel_id=1, source_target_pairs={{0,7},{1,0},{2,1},{3,2},{4,3},{5,4},{6,5},{7,6},{8,15},{9,8},{10,9... | collective-permute-start | bytes 786440 | tf_op jit(solution)/shard_map/ppermute | solution.py:129
  127.3 7.9 %collective-permute-start.13 = (bf16[128,1024]{1,0:T(8,128)(2,1)S(1)}, bf16[128,1024]{1,0:T(8,128)(2,1)S(1)}, u32[]{:S(2)}, u32[]{:S(2)}) collective-permute-start(bf16[128,1024]{1,0:T(8,128)(2,1)S(1)} %collective-permute-done.12), channel_id=1, source_target_pairs={{0,1},{1,2},{2,3},{3,4},{4,5},{5,6},{6,7},{7,0},{8,9},{9,10},{10,1... | collective-permute-start | bytes 786440 | tf_op jit(solution)/shard_map/ppermute | solution.py:126
  127.3 12.5 %collective-permute-start.10 = (bf16[128,1024]{1,0:T(8,128)(2,1)S(1)}, bf16[128,1024]{1,0:T(8,128)(2,1)S(1)}, u32[]{:S(2)}, u32[]{:S(2)}) collective-permute-start(bf16[128,1024]{1,0:T(8,128)(2,1)S(1)} %collective-permute-done.9), channel_id=1, source_target_pairs={{0,7},{1,0},{2,1},{3,2},{4,3},{5,4},{6,5},{7,6},{8,15},{9,8},{10,9... | collective-permute-start | bytes 786440 | tf_op jit(solution)/shard_map/ppermute | solution.py:129
  135.2 10.4 %collective-permute-start.14 = (bf16[128,1024]{1,0:T(8,128)(2,1)S(1)}, bf16[128,1024]{1,0:T(8,128)(2,1)S(1)}, u32[]{:S(2)}, u32[]{:S(2)}) collective-permute-start(bf16[128,1024]{1,0:T(8,128)(2,1)S(1)} %collective-permute-done.13), channel_id=1, source_target_pairs={{0,1},{1,2},{2,3},{3,4},{4,5},{5,6},{6,7},{7,0},{8,9},{9,10},{10,1... | collective-permute-start | bytes 786440 | tf_op jit(solution)/shard_map/ppermute | solution.py:126
  156.2 21.6 %collective-permute-start.15 = (bf16[128,4096]{1,0:T(8,128)(2,1)S(1)}, bf16[128,4096]{1,0:T(8,128)(2,1)S(1)}, u32[]{:S(2)}, u32[]{:S(2)}) collective-permute-start(bf16[128,4096]{1,0:T(8,128)(2,1)S(1)} %constant_dynamic-slice_fusion), channel_id=1, source_target_pairs={{0,8},{8,0},{1,9},{9,1},{2,10},{10,2},{3,11},{11,3},{4,12},{12,4},... | collective-permute-start | bytes 3145736 | tf_op jit(solution)/shard_map/ppermute | solution.py:75
  179.7 3.2 %collective-permute-start.16 = (f32[128,4,192]{0,2,1:T(8,128)S(1)}, f32[128,4,192]{0,2,1:T(8,128)S(1)}, u32[]{:S(2)}, u32[]{:S(2)}) collective-permute-start(f32[128,4,192]{0,2,1:T(8,128)S(1)} %bitcast.101), channel_id=1, source_target_pairs={{0,8},{8,0},{1,9},{9,1},{2,10},{10,2},{3,11},{11,3},{4,12},{12,4},... | collective-permute-start | bytes 1179656 | tf_op jit(solution)/shard_map/ppermute | solution.py:75
Sparse Core Ops, SparseCore 0:
  104.4 70.1 all-gather.2

commit v5 on v3

--- a/solution.py
+++ b/solution.py
@@ -132,27 +132,12 @@
     )
     attended = local_out + inherited
     hidden = normalize(attended, norm_gain, gate_logits)
-    chips, cores, groups = (lax.axis_size("chip"), lax.axis_size("core"), lax.axis_size("tensor"))
-    core = lax.axis_index("core")
-    seq_len = chips * cores
-    col_blocks = seq_len // groups
-    quarter = chips // col_blocks
-    route = []
-    for q in range(chips):
-        for c in range(cores):
-            for t in range(groups):
-                source = (col_blocks * t + q // quarter) * groups + (groups // cores) * c + q % quarter
-                route.append((source, (q * cores + c) * groups + t))
-    placed = lax.ppermute(out_weight, ("chip", "core", "tensor"), route)
-    columns = lax.all_gather(placed, "chip", axis=0, tiled=False)
-    columns = columns.reshape(col_blocks, -1, columns.shape[-1])
-    width = columns.shape[1]
-    full_hidden = lax.all_gather(hidden, "tensor", axis=1, tiled=True)
-    mine = lax.dynamic_slice_in_dim(full_hidden, core * width, width, axis=1)
-    theirs = swap_cores(lax.dynamic_slice_in_dim(full_hidden, (1 - core) * width, width, axis=1))
-    own_part = jnp.einsum("tk,rkc->trc", mine, columns, preferred_element_type=jnp.float32)
-    their_part = jnp.einsum("tk,rkc->trc", theirs, columns, preferred_element_type=jnp.float32)
-    mixed = (own_part + swap_cores(their_part)).reshape(rows_here, -1)
+    terms = jnp.dot(
+        hidden,
+        lax.all_gather(out_weight, ("chip", "core"), axis=1, tiled=True),
+        preferred_element_type=jnp.float32,
+    )
+    mixed = lax.psum_scatter(terms, "tensor", scatter_dimension=1, tiled=True)
     return mixed
 
 

time: 227 us -> 184 us (0.81)
  waiting for transfers between devices: 161 us -> 128 us
  starting transfers between devices: 30.9 us -> 23.4 us
  matrix products: 6.74 us -> 13.6 us
  local copies, waits for them, and re-layouts: 9.79 us -> 3.7 us
    ppermute x1 -> x0, waiting for transfers between devices: 48.8 us -> none  [per_device(): placed = lax.ppermute(out_weight, ('chip', 'core', 'tensor'), route)]
    reduce_scatter x0 -> x1, waiting for transfers between devices: none -> 46.8 us  [per_device(): mixed = lax.psum_scatter(terms, 'tensor', scatter_dimension=1, tiled=True)]
    all_gather x2 -> x1, waiting for transfers between devices: 85.4 us -> 54.1 us  [per_device(): lax.all_gather(out_weight, ('chip', 'core'), axis=1, tiled=True)]
    dot_general x0 -> x1, matrix products: none -> 10.5 us  [per_device(): jnp.dot(hidden, lax.all_gather(out_weight, ('chip', 'core'), axis=1, tile...]
    ppermute x1 -> x0, starting transfers between devices: 7.4 us -> none  [per_device(): placed = lax.ppermute(out_weight, ('chip', 'core', 'tensor'), route)]
    reshape x2 -> x0, local copies, waits for them, and re-layouts: 4.12 us -> none  [the longest x1 3.21 us: per_device(): columns = columns.reshape(col_blocks, -1, columns.shape[-1])]
    unnamed x2 -> x0, matrix products: 3.59 us -> none
  transfers between devices with their start and end apart: 12 -> 9, of which waited for: 10 -> 9; matrix products, arithmetic and copies ran while one was open for 3% -> 2% of each run, Pallas kernels for 0% -> 0%
where the time goes in v5:
time: 184 us
  waiting for transfers between devices  128 us (70%)
  starting transfers between devices  23.4 us (13%)
  between operations  13.7 us (7%)
  matrix products  13.6 us (7%)
  local copies, waits for them, and re-layouts  3.7 us (2%)
  other arithmetic  2.07 us (1%)
    all_gather x1, waiting for transfers between devices, per_device(): lax.all_gather(out_weight, ('chip', 'core'), axis=1, tiled=True)  54.1 us
    reduce_scatter x1, waiting for transfers between devices, per_device(): mixed = lax.psum_scatter(terms, 'tensor', scatter_dimension=1, tiled=True)  46.8 us
    ppermute x4, starting transfers between devices, carried_in(): lax.ppermute(current, 'chip', [(i, i + step) for i in range(chips - step)])  20 us
    ppermute x4, waiting for transfers between devices, carried_in(): lax.ppermute(current, 'chip', [(i, i + step) for i in range(chips - step)])  17.6 us
    dot_general x1, matrix products, per_device(): jnp.dot(hidden, lax.all_gather(out_weight, ('chip', 'core'), axis=1, tile...  10.5 us
    ppermute x1, waiting for transfers between devices, carried_in(): lax.ppermute(chip_element, 'chip', [(i, i + 1) for i in range(chips - 1)])  6.94 us
  transfers between devices with their start and end apart: 9, of which 9 were waited for; matrix products, arithmetic and copies ran while one was open for 2% of the time, Pallas kernels for 0%

profile of v5, /device:TPU:4, one launch (start us, length us, event | category | flops | bytes accessed | tf_op | source)
XLA Modules:
  0.0 184.1 jit_solution(1943625744013885073)
XLA Ops:
  6.6 0.9 copy.35
  7.8 1.1 copy.52
  8.9 1.4 fusion.4
  10.3 0.3 copy.89
  10.8 1.5 collective-permute-done
  12.8 3.1 %collective-permute-start.1 = (f32[4,16512]{1,0:T(4,128)S(1)}, f32[4,16512]{1,0:T(4,128)S(1)}, u32[]{:S(2)}, u32[]{:S(2)}) collective-permute-start(f32[4,16512]{1,0:T(4,128)S(1)} %pad_maximum_fusion.2), channel_id=1, source_target_pairs={{0,16},{16,32},{32,48},{48,64},{64,80},{80,96},{96,112},{112,128},... | collective-permute-start | bytes 792584 | tf_op jit(solution)/shard_map/ppermute | solution.py:89
  16.1 6.9 %collective-permute-done.1 = f32[4,16512]{1,0:T(4,128)S(1)} collective-permute-done((f32[4,16512]{1,0:T(4,128)S(1)}, f32[4,16512]{1,0:T(4,128)S(1)}, u32[]{:S(2)}, u32[]{:S(2)}) %collective-permute-start.1) | collective-permute-done | bytes 264224 | tf_op jit(solution)/shard_map/ppermute | solution.py:89
  23.1 3.1 %collective-permute-start.2 = (f32[4,16512]{1,0:T(4,128)S(1)}, f32[4,16512]{1,0:T(4,128)S(1)}, u32[]{:S(2)}, u32[]{:S(2)}) collective-permute-start(f32[4,16512]{1,0:T(4,128)S(1)} %pad_select_fusion), channel_id=1, source_target_pairs={{0,16},{16,32},{32,48},{48,64},{64,80},{80,96},{96,112},{112,128},... | collective-permute-start | bytes 792584 | tf_op jit(solution)/shard_map/ppermute | solution.py:95
  26.4 6.2 %collective-permute-done.2 = f32[4,16512]{1,0:T(4,128)S(1)} collective-permute-done((f32[4,16512]{1,0:T(4,128)S(1)}, f32[4,16512]{1,0:T(4,128)S(1)}, u32[]{:S(2)}, u32[]{:S(2)}) %collective-permute-start.2) | collective-permute-done | bytes 264224 | tf_op jit(solution)/shard_map/ppermute | solution.py:95
  32.8 7.6 %collective-permute-start.3 = (f32[4,16512]{1,0:T(4,128)S(1)}, f32[4,16512]{1,0:T(4,128)S(1)}, u32[]{:S(2)}, u32[]{:S(2)}) collective-permute-start(f32[4,16512]{1,0:T(4,128)S(1)} %maximum_select_fusion), channel_id=1, source_target_pairs={{0,32},{16,48},{32,64},{48,80},{64,96},{80,112},{96,128},{112,144}... | collective-permute-start | bytes 792584 | tf_op jit(solution)/shard_map/ppermute | solution.py:95
  40.6 4.1 %collective-permute-done.3 = f32[4,16512]{1,0:T(4,128)S(1)} collective-permute-done((f32[4,16512]{1,0:T(4,128)S(1)}, f32[4,16512]{1,0:T(4,128)S(1)}, u32[]{:S(2)}, u32[]{:S(2)}) %collective-permute-start.3) | collective-permute-done | bytes 264224 | tf_op jit(solution)/shard_map/ppermute | solution.py:95
  44.9 3.5 %collective-permute-start.4 = (f32[4,16512]{1,0:T(4,128)S(1)}, f32[4,16512]{1,0:T(4,128)S(1)}, u32[]{:S(2)}, u32[]{:S(2)}) collective-permute-start(f32[4,16512]{1,0:T(4,128)S(1)} %maximum_select_fusion.1), channel_id=1, source_target_pairs={{0,64},{16,80},{32,96},{48,112},{64,128},{80,144},{96,160},{112,17... | collective-permute-start | bytes 792584 | tf_op jit(solution)/shard_map/ppermute | solution.py:95
  48.6 3.7 %collective-permute-done.4 = f32[4,16512]{1,0:T(4,128)S(1)} collective-permute-done((f32[4,16512]{1,0:T(4,128)S(1)}, f32[4,16512]{1,0:T(4,128)S(1)}, u32[]{:S(2)}, u32[]{:S(2)}) %collective-permute-start.4) | collective-permute-done | bytes 264224 | tf_op jit(solution)/shard_map/ppermute | solution.py:95
  52.5 5.8 %collective-permute-start.5 = (f32[4,16512]{1,0:T(4,128)S(1)}, f32[4,16512]{1,0:T(4,128)S(1)}, u32[]{:S(2)}, u32[]{:S(2)}) collective-permute-start(f32[4,16512]{1,0:T(4,128)S(1)} %maximum_select_fusion.2), channel_id=1, source_target_pairs={{0,128},{16,144},{32,160},{48,176},{64,192},{80,208},{96,224},{112... | collective-permute-start | bytes 792584 | tf_op jit(solution)/shard_map/ppermute | solution.py:95
  58.5 3.6 %collective-permute-done.5 = f32[4,16512]{1,0:T(4,128)S(1)} collective-permute-done((f32[4,16512]{1,0:T(4,128)S(1)}, f32[4,16512]{1,0:T(4,128)S(1)}, u32[]{:S(2)}, u32[]{:S(2)}) %collective-permute-start.5) | collective-permute-done | bytes 264224 | tf_op jit(solution)/shard_map/ppermute | solution.py:95
  62.9 0.7 fusion.2
  63.6 0.7 collective-permute-done.6
  64.3 0.2 fusion.9
  64.5 0.6 fusion.3
  65.1 0.5 multiply_reduce_fusion
  65.7 0.2 copy.49
  65.9 54.1 %all-gather.2.cloned.1.call-done = bf16[1024,6144]{0,1:T(8,128)(2,1)} async-done(((bf16[1024,192]{0,1:T(8,128)(2,1)}), bf16[1024,6144]{0,1:T(8,128)(2,1)}) %all-gather.2.cloned.1.call-update) | async-done | bytes 12582928 | tf_op jit(solution)/shard_map/all_gather | solution.py:137
  119.9 10.5 %fusion.18 = f32[128,6144]{1,0:T(8,128)} fusion(bf16[1024,6144]{0,1:T(8,128)(2,1)} %all-gather.2.cloned.1.call-done, bf16[128,1024]{1,0:T(8,128)(2,1)S(1)} %copy-done.3, f32[128,1024]{1,0:T(8,128)S(1)} %copy.49, f32[1024]{0:T(1024)S(1)} %copy-done.4), kind=kOutput, calls=%fused_computation.39 | convolution fusion | flops 1611530240 | bytes 16519168 | tf_op jit(solution)/shard_map/dot_general | solution.py:135
  130.4 46.8 %reduce-scatter.2.cloned.1.call-done = f32[128,768]{1,0:T(8,128)} async-done(((f32[128,6144]{1,0:T(8,128)}), f32[128,768]{1,0:T(8,128)}) %reduce-scatter.2.cloned.1.call-update) | async-done | bytes 393232 | tf_op jit(solution)/shard_map/reduce_scatter | solution.py:140
  (56 shorter events, 3.3 us)
Async XLA Ops:
  6.5 9.4 %copy-start = (f32[8,128,128]{2,1,0:T(8,128)S(1)}, f32[8,128,128]{2,1,0:T(8,128)}, u32[]{:S(2)}) copy-start(f32[8,128,128]{2,1,0:T(8,128)} %param.13) | copy-start | bytes 1572868
  6.5 58.5 %copy-start.2 = (bf16[128,1024]{1,0:T(8,128)(2,1)S(1)}, bf16[128,1024]{1,0:T(8,128)(2,1)}, u32[]{:S(2)}) copy-start(bf16[128,1024]{1,0:T(8,128)(2,1)} %param.10) | copy-start | bytes 786436
  6.5 56.4 %copy-start.1 = (bf16[128,1024]{1,0:T(8,128)(2,1)S(1)}, bf16[128,1024]{1,0:T(8,128)(2,1)}, u32[]{:S(2)}) copy-start(bf16[128,1024]{1,0:T(8,128)(2,1)} %param.8) | copy-start | bytes 786436
  6.5 113.4 %copy-start.4 = (f32[1024]{0:T(1024)S(1)}, f32[1024]{0:T(1024)}, u32[]{:S(2)}) copy-start(f32[1024]{0:T(1024)} %param.14) | copy-start | bytes 12292
  6.5 113.4 %copy-start.3 = (bf16[128,1024]{1,0:T(8,128)(2,1)S(1)}, bf16[128,1024]{1,0:T(8,128)(2,1)}, u32[]{:S(2)}) copy-start(bf16[128,1024]{1,0:T(8,128)(2,1)} %param.11) | copy-start | bytes 786436
  6.5 113.4 %all-gather.2.cloned.1.call-start = ((), (), s32[]{:S(2)}) async-start(), calls=%async_computation.1 | async-start | bytes 12976128 | tf_op jit(solution)/shard_map/all_gather | solution.py:137
  10.7 1.6 collective-permute-start
  12.8 10.3 %collective-permute-start.1 = (f32[4,16512]{1,0:T(4,128)S(1)}, f32[4,16512]{1,0:T(4,128)S(1)}, u32[]{:S(2)}, u32[]{:S(2)}) collective-permute-start(f32[4,16512]{1,0:T(4,128)S(1)} %pad_maximum_fusion.2), channel_id=1, source_target_pairs={{0,16},{16,32},{32,48},{48,64},{64,80},{80,96},{96,112},{112,128},... | collective-permute-start | bytes 792584 | tf_op jit(solution)/shard_map/ppermute | solution.py:89
  23.1 9.4 %collective-permute-start.2 = (f32[4,16512]{1,0:T(4,128)S(1)}, f32[4,16512]{1,0:T(4,128)S(1)}, u32[]{:S(2)}, u32[]{:S(2)}) collective-permute-start(f32[4,16512]{1,0:T(4,128)S(1)} %pad_select_fusion), channel_id=1, source_target_pairs={{0,16},{16,32},{32,48},{48,64},{64,80},{80,96},{96,112},{112,128},... | collective-permute-start | bytes 792584 | tf_op jit(solution)/shard_map/ppermute | solution.py:95
  32.8 11.8 %collective-permute-start.3 = (f32[4,16512]{1,0:T(4,128)S(1)}, f32[4,16512]{1,0:T(4,128)S(1)}, u32[]{:S(2)}, u32[]{:S(2)}) collective-permute-start(f32[4,16512]{1,0:T(4,128)S(1)} %maximum_select_fusion), channel_id=1, source_target_pairs={{0,32},{16,48},{32,64},{48,80},{64,96},{80,112},{96,128},{112,144}... | collective-permute-start | bytes 792584 | tf_op jit(solution)/shard_map/ppermute | solution.py:95
  44.9 7.4 %collective-permute-start.4 = (f32[4,16512]{1,0:T(4,128)S(1)}, f32[4,16512]{1,0:T(4,128)S(1)}, u32[]{:S(2)}, u32[]{:S(2)}) collective-permute-start(f32[4,16512]{1,0:T(4,128)S(1)} %maximum_select_fusion.1), channel_id=1, source_target_pairs={{0,64},{16,80},{32,96},{48,112},{64,128},{80,144},{96,160},{112,17... | collective-permute-start | bytes 792584 | tf_op jit(solution)/shard_map/ppermute | solution.py:95
  48.4 128.8 %reduce-scatter.2.cloned.1.call-start = ((), (), s32[]{:S(2)}) async-start(), calls=%async_computation.2 | async-start | bytes 3538944 | tf_op jit(solution)/shard_map/reduce_scatter | solution.py:140
  52.5 9.6 %collective-permute-start.5 = (f32[4,16512]{1,0:T(4,128)S(1)}, f32[4,16512]{1,0:T(4,128)S(1)}, u32[]{:S(2)}, u32[]{:S(2)}) collective-permute-start(f32[4,16512]{1,0:T(4,128)S(1)} %maximum_select_fusion.2), channel_id=1, source_target_pairs={{0,128},{16,144},{32,160},{48,176},{64,192},{80,208},{96,224},{112... | collective-permute-start | bytes 792584 | tf_op jit(solution)/shard_map/ppermute | solution.py:95
  62.7 1.6 collective-permute-start.6
Sparse Core Ops, SparseCore 0:
  48.5 71.3 all-gather.1
  130.5 46.6 reduce-scatter.1
